TPU v7x, 256 devices: a whole 4x4x8 slice. The times are simulated.
256 devices in a mesh: tm: 32 (over y, z), weight: 8 (over x, core).
Axes of the slice: x: 4, y: 4, z: 8, core: 2. Of those that a mesh axis runs over, the one named last changes fastest.
Arguments:
- tokens: bfloat16 [32768, 2560], P(('tm', 'weight')), may hold values from -6 to 6
- segments: int32 [32768], P('tm'), may hold values from 0 to 31, never falling along the last dimension, each value on 1 to 3072 neighbouring positions
- w_z: bfloat16 [2560, 3072], P(None, 'weight'), may hold values from -0.125 to 0.125
- w_x: bfloat16 [2560, 3072], P(None, 'weight'), may hold values from -0.125 to 0.125
- w_dt: bfloat16 [2560, 48], P(None, 'weight'), may hold values from -0.125 to 0.125
- w_bc: bfloat16 [2560, 256], replicated, may hold values from -0.125 to 0.125
- conv_x: float32 [4, 3072], P(None, 'weight'), may hold values from -2.5 to 2.5
- conv_bc: float32 [4, 256], replicated, may hold values from -2.5 to 2.5
- dt_bias: float32 [48], P('weight'), may hold values from -3 to -1
- decay_rate: float32 [48], P('weight'), may hold values from 0 to 1.5
- skip_d: float32 [48], P('weight'), may hold values from 0.5 to 1.5
- norm_gain: bfloat16 [3072], P('weight'), may hold values from 0.5 to 1.5
- w_out: bfloat16 [3072, 2560], P('weight'), may hold values from -0.109375 to 0.109375
Outputs:
- mixed: bfloat16 [32768, 2560], P(('tm', 'weight'))
Inputs may be any that keep to these rules, and one draw needn't show every extreme that they name: `segments`: document numbers never fall along the stream; a document has at most 3072 frames.
All inputs are finite; a program needn't handle non-finite values.
Results may differ from a plain program's by a relative error of at most 0.015.
Values may be sent and summed in bfloat16 or wider, within the bound.
A program may use at most 64 MiB of HBM per device.

v0:
```python
import jax
import jax.numpy as jnp
from jax import lax
from jax.sharding import PartitionSpec as P

GROUP = 256


eps_norm = 1e-05


def passed_along(block, axis, distance):
    devices = range(lax.axis_size(axis))
    route = [(i - distance, i) for i in devices if i - distance in devices]
    return lax.ppermute(block, axis, route)


def entering(shard, axis, combine, identity):
    devices, place = (lax.axis_size(axis), lax.axis_index(axis))
    everything = jax.tree.map(
        lambda part, kind: lax.all_gather(part.astype(kind), axis),
        shard,
        (jnp.bfloat16, jnp.bfloat16),
    )
    start = jax.tree.map(
        lambda part, zero: jnp.broadcast_to(jnp.asarray(zero, part.dtype), part.shape),
        shard,
        identity,
    )

    def step(k, before):
        reached = k < place
        new = combine(
            before, jax.tree.map(lambda part, own: part[k].astype(own.dtype), everything, shard)
        )
        return jax.tree.map(lambda a, b: jnp.where(reached, a, b), new, before)

    return lax.fori_loop(0, devices, step, start)


def conv_rows(xbc, seg, prev_xbc, prev_seg, conv_w):
    full = jnp.concatenate([prev_xbc, xbc], 0).astype(jnp.float32)
    segs = jnp.concatenate([prev_seg, seg], 0)
    count = xbc.shape[0]
    total = jnp.zeros(xbc.shape, jnp.float32)
    for k in range(4):
        same = (segs[k : k + count] == seg).astype(jnp.float32)
        total = total + full[k : k + count] * conv_w[k][None, :] * same[:, None]
    return jax.nn.silu(total)


def group_ssd(xs, dts, rate, bmat, cmat, seg, ssm, seg_in):
    size = seg.shape[0]
    logs = jnp.cumsum(-dts * rate[None, :], axis=0)
    order = jnp.arange(size)
    lower = (order[:, None] >= order[None, :]) & (seg[:, None] == seg[None, :])
    scores = jnp.dot(cmat, bmat.T, preferred_element_type=jnp.float32)
    diff = jnp.minimum(logs[:, None, :] - logs[None, :, :], 0.0)
    mix = jnp.where(lower[:, :, None], jnp.exp(diff), 0.0) * scores[:, :, None] * dts[None, :, :]
    mix = mix.astype(jnp.bfloat16)
    inner = jnp.einsum("ijh,jhp->ihp", mix, xs, preferred_element_type=jnp.float32)
    enter = jnp.exp(logs) * (seg == seg_in).astype(jnp.float32)[:, None]
    carried = (
        jnp.einsum("in,hnp->ihp", cmat.astype(jnp.float32), ssm, precision=lax.Precision.HIGHEST)
        * enter[:, :, None]
    )
    tail = jnp.exp(logs[-1][None, :] - logs) * (seg == seg[-1]).astype(jnp.float32)[:, None] * dts
    scaled = (xs.astype(jnp.float32) * tail[:, :, None]).astype(jnp.bfloat16)
    fresh = jnp.einsum("jn,jhp->hnp", bmat, scaled, preferred_element_type=jnp.float32)
    keep = jnp.exp(logs[-1]) * (seg[-1] == seg_in).astype(jnp.float32)
    return (inner + carried, ssm * keep[:, None, None] + fresh)


def chain(early, later):
    return (early[0] * later[0], early[1] * later[0][:, None, None] + later[1])


def on_device(
    tokens,
    segments,
    w_z,
    w_x,
    w_dt,
    w_bc,
    conv_x,
    conv_bc,
    dt_bias,
    decay_rate,
    skip_d,
    norm_gain,
    w_out,
):
    heads = decay_rate.shape[0]
    width_dev = w_x.shape[1]
    head_dim = width_dev // heads
    state = w_bc.shape[1] // 2
    panel = jnp.concatenate([w_z, w_x, w_bc, w_dt], axis=1)
    proj = jnp.dot(
        lax.all_gather(tokens, "weight", axis=0, tiled=True),
        panel,
        preferred_element_type=jnp.float32,
    ).astype(jnp.bfloat16)
    block = proj.shape[0]
    gate_z = proj[:, :width_dev]
    xbc = proj[:, width_dev : 2 * width_dev + 2 * state]
    dt_raw = proj[:, 2 * width_dev + 2 * state :]
    prev_xbc, prev_segf = passed_along((xbc[-3:], segments[-3:].astype(jnp.bfloat16)), "tm", 1)
    prev_seg = prev_segf.astype(jnp.int32)
    seg_in = prev_seg[-1]
    conv_w = jnp.concatenate([conv_x, conv_bc], axis=1)
    conv = conv_rows(xbc, segments, prev_xbc, prev_seg, conv_w).astype(jnp.bfloat16)
    xs = conv[:, :width_dev].reshape(block, heads, head_dim)
    bmat = conv[:, width_dev : width_dev + state]
    cmat = conv[:, width_dev + state :]
    dts = jax.nn.softplus(dt_raw.astype(jnp.float32) + dt_bias[None, :])
    count = block // GROUP

    def advance(carry, inputs):
        ssm, entry = carry
        x_part, d_part, b_part, c_part, s_part = inputs
        ys, ssm_next = group_ssd(x_part, d_part, decay_rate, b_part, c_part, s_part, ssm, entry)
        return ((ssm_next, s_part[-1]), ys)

    start = (jnp.zeros((heads, state, head_dim), jnp.float32), seg_in)
    pieces = (
        xs.reshape(count, GROUP, heads, head_dim),
        dts.reshape(count, GROUP, heads),
        bmat.reshape(count, GROUP, state),
        cmat.reshape(count, GROUP, state),
        segments.reshape(count, GROUP),
    )
    final, ys = lax.scan(advance, start, pieces)
    local_state = final[0]
    ys = ys.reshape(block, heads, head_dim)
    block_logs = jnp.cumsum(-dts * decay_rate[None, :], axis=0)
    local_decay = jnp.exp(block_logs[-1]) * (segments[-1] == seg_in).astype(jnp.float32)
    unit = (jnp.ones((heads,), jnp.float32), jnp.zeros((heads, state, head_dim), jnp.float32))
    carry_decay, carry_state = entering((local_decay, local_state), "tm", chain, unit)
    enter = jnp.exp(block_logs) * (segments == seg_in).astype(jnp.float32)[:, None]
    carried = (
        jnp.einsum(
            "in,hnp->ihp", cmat.astype(jnp.float32), carry_state, precision=lax.Precision.HIGHEST
        )
        * enter[:, :, None]
    )
    ys = ys + carried + skip_d[None, :, None] * xs.astype(jnp.float32)
    gated = ys.reshape(block, width_dev) * jax.nn.silu(gate_z.astype(jnp.float32))
    total_width = width_dev * lax.axis_size("weight")
    squares = lax.psum(jnp.sum(gated * gated, axis=1), "weight")
    inverse = lax.rsqrt(squares / total_width + eps_norm)
    normed = (gated * inverse[:, None] * norm_gain.astype(jnp.float32)[None, :]).astype(
        jnp.bfloat16
    )
    return lax.psum_scatter(
        jnp.dot(normed, w_out, preferred_element_type=jnp.float32).astype(jnp.bfloat16),
        "weight",
        scatter_dimension=0,
        tiled=True,
    )


def solution(mesh):
    return jax.shard_map(
        on_device,
        mesh=mesh,
        in_specs=(
            P(("tm", "weight"), None),
            P("tm"),
            P(None, "weight"),
            P(None, "weight"),
            P(None, "weight"),
            P(),
            P(None, "weight"),
            P(),
            P("weight"),
            P("weight"),
            P("weight"),
            P("weight"),
            P("weight", None),
        ),
        out_specs=P(("tm", "weight"), None),
        check_vma=False,
    )
```

profile of v0, /device:TPU:25, one launch (start us, length us, event | category | flops | bytes accessed | tf_op | source)
XLA Modules:
  0.0 347.5 jit_solution(2320911016319990322)
XLA Ops:
  8.1 3.5 %collective-permute-start = (bf16[3]{0:T(256)(128)(2,1)S(1)}, bf16[3]{0:T(256)(128)(2,1)S(1)}, u32[]{:S(2)}, u32[]{:S(2)}) collective-permute-start(bf16[3]{0:T(256)(128)(2,1)S(1)} %slice.90), channel_id=1, source_target_pairs={{0,8},{8,16},{16,24},{24,32},{32,40},{40,48},{48,56},{56,64},{64,7... | collective-permute-start | bytes 26 | tf_op jit(solution)/shard_map/ppermute | solution.py:15
  14.9 1.8 collective-permute-done
  17.9 1.5 fusion.67
  19.5 31.8 %all-gather.5.cloned.1.call-done = bf16[1024,2560]{1,0:T(8,128)(2,1)} async-done(((bf16[128,2560]{1,0:T(8,128)(2,1)}), bf16[1024,2560]{1,0:T(8,128)(2,1)}) %all-gather.5.cloned.1.call-update) | async-done | bytes 5242896 | tf_op jit(solution)/shard_map/all_gather | solution.py:99
  51.3 10.4 %fusion.43 = bf16[1024,1030]{0,1:T(8,128)(2,1)S(1)} fusion(bf16[1024,2560]{1,0:T(8,128)(2,1)} %all-gather.5.cloned.1.call-done, bf16[2560,6]{1,0:T(8,128)(2,1)S(1)} %copy.93, bf16[2560,256]{1,0:T(8,128)(2,1)} %param.22, bf16[2560,384]{1,0:T(8,128)(2,1)} %param.20, bf16[2560,384]{1,0:T(8,128)(2,1)} %param.19), kind=kOutput, calls=%fused_computation.61 | convolution fusion | flops 5422315520 | bytes 12625920 | tf_op jit(solution)/shard_map/dot_general | solution.py:98
  61.9 3.4 collective-permute-start.1
  65.5 5.9 %collective-permute-done.1 = bf16[3,640]{0,1:T(8,128)(2,1)S(1)} collective-permute-done((bf16[3,640]{0,1:T(8,128)(2,1)S(1)}, bf16[3,640]{0,1:T(8,128)(2,1)S(1)}, u32[]{:S(2)}, u32[]{:S(2)}) %collective-permute-start.1) | collective-permute-done | bytes 3872 | tf_op jit(solution)/shard_map/ppermute | solution.py:15
  72.1 2.9 multiply_convert_fusion.3
  77.6 2.2 copy.95
  81.4 80.7 %while.29 = (s32[]{:T(128)}, f32[6,128,64]{1,2,0:T(8,128)S(1)}, s32[]{:T(128)}, f32[4,256,6,64]{1,0,3,2:T(4,128)}, f32[4,256,6]{1,2,0:T(8,128)S(1)}, /*index=5*/...) while((s32[]{:T(128)}, f32[6,128,64]{1,2,0:T(8,128)S(1)}, ...), condition=%wide.region_3.4_spmd.clone, body=%wide.region_0.3_spmd.clone.sunk | while | flops 246671392 | bytes 5188541 | solution.py:132
  82.7 1.8 reduce-window.26
  89.4 1.6 fusion.103
  91.4 9.6 %dynamic_update_slice.6 = f32[4,256,6,64]{1,0,3,2:T(4,128)} dynamic-update-slice(f32[4,256,6,64]{1,0,3,2:T(4,128)} %get-tuple-element.447, f32[1,256,6,64]{1,0,3,2:T(1,128)S(1)} %copy.141, s32[]{:T(128)S(6)} %copy.149, s32[]{:T(128)} %constant.64.clone.1..sunk, s32[]{:T(128)} %constant.64.clone.1..sunk, s32[]{:T(128)} %constant.64.clone.1..sunk) | dynamic-update-slice | bytes 786436 | tf_op jit(solution)/shard_map/while/body/jit(dynamic_update_index_in_dim)/dynamic_update_slice | solution.py:132
  102.9 1.8 reduce-window.26
  109.6 1.6 fusion.103
  111.6 9.6 %dynamic_update_slice.6 = f32[4,256,6,64]{1,0,3,2:T(4,128)} dynamic-update-slice(f32[4,256,6,64]{1,0,3,2:T(4,128)} %get-tuple-element.447, f32[1,256,6,64]{1,0,3,2:T(1,128)S(1)} %copy.141, s32[]{:T(128)S(6)} %copy.149, s32[]{:T(128)} %constant.64.clone.1..sunk, s32[]{:T(128)} %constant.64.clone.1..sunk, s32[]{:T(128)} %constant.64.clone.1..sunk) | dynamic-update-slice | bytes 786436 | tf_op jit(solution)/shard_map/while/body/jit(dynamic_update_index_in_dim)/dynamic_update_slice | solution.py:132
  123.1 1.8 reduce-window.26
  129.7 1.6 fusion.103
  131.7 9.6 %dynamic_update_slice.6 = f32[4,256,6,64]{1,0,3,2:T(4,128)} dynamic-update-slice(f32[4,256,6,64]{1,0,3,2:T(4,128)} %get-tuple-element.447, f32[1,256,6,64]{1,0,3,2:T(1,128)S(1)} %copy.141, s32[]{:T(128)S(6)} %copy.149, s32[]{:T(128)} %constant.64.clone.1..sunk, s32[]{:T(128)} %constant.64.clone.1..sunk, s32[]{:T(128)} %constant.64.clone.1..sunk) | dynamic-update-slice | bytes 786436 | tf_op jit(solution)/shard_map/while/body/jit(dynamic_update_index_in_dim)/dynamic_update_slice | solution.py:132
  143.3 1.8 reduce-window.26
  149.9 1.6 fusion.103
  151.9 9.6 %dynamic_update_slice.6 = f32[4,256,6,64]{1,0,3,2:T(4,128)} dynamic-update-slice(f32[4,256,6,64]{1,0,3,2:T(4,128)} %get-tuple-element.447, f32[1,256,6,64]{1,0,3,2:T(1,128)S(1)} %copy.141, s32[]{:T(128)S(6)} %copy.149, s32[]{:T(128)} %constant.64.clone.1..sunk, s32[]{:T(128)} %constant.64.clone.1..sunk, s32[]{:T(128)} %constant.64.clone.1..sunk) | dynamic-update-slice | bytes 786436 | tf_op jit(solution)/shard_map/while/body/jit(dynamic_update_index_in_dim)/dynamic_update_slice | solution.py:132
  165.3 1.7 reduce-window.16
  167.6 30.7 %all-gather.1 = bf16[32,1,6]{2,1,0:T(2,128)(2,1)S(1)} all-gather(bf16[1,1,6]{2,1,0:T(2,128)(2,1)S(1)} %bitcast.174), channel_id=1, replica_groups=mesh['tm'=32,'weight'=8] {'tm'}, dimensions={0}, use_global_device_ids=true | all-gather | bytes 396 | tf_op jit(solution)/shard_map/all_gather | solution.py:21
  198.4 2.9 reshape.139
  201.3 35.3 %all-gather.7.cloned.1.call-done = bf16[192,128,64]{1,2,0:T(8,128)(2,1)} async-done(((bf16[6,128,64]{1,2,0:T(8,128)(2,1)}), bf16[192,128,64]{1,2,0:T(8,128)(2,1)}) %all-gather.7.cloned.1.call-update) | async-done | bytes 3145744 | tf_op jit(solution)/shard_map/all_gather | solution.py:21
  236.6 40.1 %while.30 = (s32[]{:T(128)}, f32[6,128,64]{2,1,0:T(8,128)S(1)}, s32[]{:T(128)}, bf16[32,6]{1,0:T(8,128)(2,1)S(1)}, bf16[32,6,128,64]{2,3,1,0:T(8,128)(2,1)}, /*index=5*/s32[]{:T(128)}, s32[]{:T(128)}) while((s32[]{:T(128)}, f32[6,128,64]{2,1,0:T(8,128)S(1)}, s32[]{:T(128)}, bf16[32,6]{1,0:T(8,128)(2,1)S(1)}, ...), condition=%wide.region_7.8_spmd.clone, body=%wide.region_6.7_spmd.clone.sunk | while | flops 245770 | bytes 884909 | solution.py:38
  276.9 1.8 fusion.71
  279.3 2.9 multiply_reduce_fusion
  282.2 16.2 %psum.7 = f32[1024]{0:T(1024)S(1)} all-reduce(f32[1024]{0:T(1024)S(1)} %get-tuple-element.312), channel_id=1, replica_groups=mesh['tm'=32,'weight'=8] {'weight'}, use_global_device_ids=true, to_apply=%region_9.10 | all-reduce | flops 1024 | bytes 8192 | tf_op jit(solution)/shard_map/psum | solution.py:149
  298.4 6.3 %convolution_convert_fusion = bf16[1024,2560]{1,0:T(8,128)(2,1)} fusion(bf16[384,2560]{1,0:T(8,128)(2,1)S(1)} %copy-done, f32[1024,384]{0,1:T(8,128)} %get-tuple-element.313, f32[384]{0:T(512)S(1)} %convert_element_type.131, f32[1024]{0:T(1024)S(1)} %add_rsqrt_fusion), kind=kOutput, calls=%fused_computation.59 | convolution fusion | flops 2017067008 | bytes 8787456 | tf_op jit(solution)/shard_map/dot_general | solution.py:155
  304.7 36.3 %reduce-scatter.2.cloned.1.call-done = bf16[128,2560]{1,0:T(8,128)(2,1)} async-done(((bf16[1024,2560]{1,0:T(8,128)(2,1)}), bf16[128,2560]{1,0:T(8,128)(2,1)}) %reduce-scatter.2.cloned.1.call-update) | async-done | bytes 655376 | tf_op jit(solution)/shard_map/reduce_scatter | solution.py:154
  (269 shorter events, 76.5 us)
Async XLA Ops:
  6.5 291.9 %copy-start = (bf16[384,2560]{1,0:T(8,128)(2,1)S(1)}, bf16[384,2560]{1,0:T(8,128)(2,1)}, u32[]{:S(2)}) copy-start(bf16[384,2560]{1,0:T(8,128)(2,1)} %param.29) | copy-start | bytes 5898244
  6.5 44.7 %all-gather.5.cloned.1.call-start = ((), (), s32[]{:S(2)}) async-start(), calls=%async_computation.1 | async-start | bytes 5898240 | tf_op jit(solution)/shard_map/all_gather | solution.py:99
  7.3 229.3 %all-gather.7.cloned.1.call-start = ((), (), s32[]{:S(2)}) async-start(), calls=%async_computation.3 | async-start | bytes 3244032 | tf_op jit(solution)/shard_map/all_gather | solution.py:21
  8.1 8.6 %collective-permute-start = (bf16[3]{0:T(256)(128)(2,1)S(1)}, bf16[3]{0:T(256)(128)(2,1)S(1)}, u32[]{:S(2)}, u32[]{:S(2)}) collective-permute-start(bf16[3]{0:T(256)(128)(2,1)S(1)} %slice.90), channel_id=1, source_target_pairs={{0,8},{8,16},{16,24},{24,32},{32,40},{40,48},{48,56},{56,64},{64,7... | collective-permute-start | bytes 26 | tf_op jit(solution)/shard_map/ppermute | solution.py:15
  19.5 45.8 %copy-start.4 = (f32[6]{0:T(128)S(1)}, f32[6]{0:T(128)}, u32[]{:S(2)}) copy-start(f32[6]{0:T(128)} %param.26) | copy-start | bytes 76
  19.5 45.8 %copy-start.7 = (f32[6]{0:T(128)S(1)}, f32[6]{0:T(128)}, u32[]{:S(2)}) copy-start(f32[6]{0:T(128)} %param.25) | copy-start | bytes 76
  61.7 10.3 %copy-start.3 = (bf16[1024,1030]{0,1:T(8,128)(2,1)}, bf16[1024,1030]{0,1:T(8,128)(2,1)S(1)}, u32[]{:S(2)}) copy-start(bf16[1024,1030]{0,1:T(8,128)(2,1)S(1)} %fusion.43) | copy-start | bytes 6328324
  61.9 9.5 %collective-permute-start.1 = (bf16[3,640]{0,1:T(8,128)(2,1)S(1)}, bf16[3,640]{0,1:T(8,128)(2,1)S(1)}, u32[]{:S(2)}, u32[]{:S(2)}) collective-permute-start(bf16[3,640]{0,1:T(8,128)(2,1)S(1)} %slice.121), channel_id=1, source_target_pairs={{0,8},{8,16},{16,24},{24,32},{32,40},{40,48},{48,56},{56,64},{64,7... | collective-permute-start | bytes 11528 | tf_op jit(solution)/shard_map/ppermute | solution.py:15
  74.9 1.2 copy-start.1
  81.4 82.7 %copy-start.5 = (bf16[384]{0:T(512)(128)(2,1)S(1)}, bf16[384]{0:T(512)(128)(2,1)}, u32[]{:S(2)}) copy-start(bf16[384]{0:T(512)(128)(2,1)} %param.28) | copy-start | bytes 2308
  162.8 178.2 %reduce-scatter.2.cloned.1.call-start = ((), (), s32[]{:S(2)}) async-start(), calls=%async_computation.2 | async-start | bytes 5898240 | tf_op jit(solution)/shard_map/reduce_scatter | solution.py:154
  276.7 2.0 copy-start.6
  276.8 1.9 copy-start.2
Sparse Core Ops, SparseCore 0:
  9.2 42.0 all-gather.4
  162.9 73.6 all-gather.6
  304.9 36.0 reduce-scatter.1
where the time goes:
time: 353 us; the launch traced here: 348 us
  waiting for transfers between devices  112 us (32%)
  local copies, waits for them, and re-layouts  93.8 us (27%)
  blocking collectives  46.9 us (13%)
  matrix products  38.5 us (11%)
  other arithmetic  27.9 us (8%)
  between operations  15.2 us (4%)
  starting transfers between devices  6.98 us (2%)
  loops' own time  6.59 us (2%)
    dynamic_update_slice x8, local copies, waits for them, and re-layouts, on_device(): final, ys = lax.scan(advance, start, pieces)  39.8 us
    reduce_scatter x1, waiting for transfers between devices, on_device(): lax.psum_scatter(jnp.dot(normed, w_out, preferred_element_type=jnp.float3...  36.3 us
    all_gather x1, waiting for transfers between devices, entering(): lax.all_gather(part.astype(kind), axis)  35.3 us
    dynamic_slice x64, local copies, waits for them, and re-layouts, step(): part[k].astype(own.dtype)  34.4 us
    all_gather x1, waiting for transfers between devices, on_device(): lax.all_gather(tokens, 'weight', axis=0, tiled=True)  31.8 us
    all_gather x1, blocking collectives, entering(): lax.all_gather(part.astype(kind), axis)  30.7 us
    psum x1, blocking collectives, on_device(): squares = lax.psum(jnp.sum(gated * gated, axis=1), 'weight')  16.2 us
    dot_general x1, matrix products, on_device(): jnp.dot(lax.all_gather(tokens, 'weight', axis=0, tiled=True), panel, pref...  10.4 us
  transfers between devices with their start and end apart: 5, of which 5 were waited for; matrix products, arithmetic and copies ran while one was open for 4% of the time, Pallas kernels for 0%

commit v1 on v0

v1 whole, which is shorter than its diff:
```python
import functools

import jax
import jax.numpy as jnp
from jax import lax
from jax.experimental import pallas as pl
from jax.experimental.pallas import tpu as pltpu
from jax.sharding import PartitionSpec as P

GROUP = 256
LANES = 128
HALO = 16
EPS = 1e-5
F32 = jnp.float32
BF16 = jnp.bfloat16
MESH = pl.DeviceIdType.MESH
VMEM_LIMIT = 60 * 1024 * 1024


def whole(space=pltpu.VMEM):
    return pl.BlockSpec(memory_space=space)


def here():
    w = lax.axis_index("weight")
    return lax.axis_index("tm"), lax.div(w, 2), lax.rem(w, 2)


def at(t, x, c):
    return {"tm": t, "weight": x * 2 + c}


def greet(senders, receivers_count):
    barrier = pltpu.get_barrier_semaphore()
    for device in senders:
        pl.semaphore_signal(barrier, inc=1, device_id=device, device_id_type=MESH)
    pl.semaphore_wait(barrier, receivers_count)


def remote(src, dst, send, recv, device):
    return pltpu.make_async_remote_copy(
        src_ref=src, dst_ref=dst, send_sem=send, recv_sem=recv, device_id=device, device_id_type=MESH
    )


def mm(a, b):
    return jnp.dot(a, b, preferred_element_type=F32)


def gather_kernel(
    nx, nt, tok, seg, wz, wx, wbc, wdt, wo,
    z_out, xbc_out, dt_out, halo_out, seg_out, wo_out,
    buf, wzx_v, wbc_v, wdt_v, halo_s, seg_s, send, recv, local,
):
    t, x, c = here()
    rows = tok.shape[0]
    half = rows // 2
    width = wz.shape[1]
    right = at(t, lax.rem(x + 1, nx), c)
    left = at(t, lax.rem(x + nx - 1, nx), c)
    mate = at(t, x, 1 - c)
    after = at(lax.rem(t + 1, nt), x, c)
    before = at(lax.rem(t + nt - 1, nt), x, c)

    def chunk(xx, cc, start=0, size=rows):
        begin = (lax.rem(xx + nx, nx) * 2 + cc) * rows + start
        return buf.at[pl.ds(pl.multiple_of(begin, half), size)]

    own = pltpu.make_async_copy(tok, chunk(x, c), local.at[0])
    own.start()
    greet((right, left, mate, before), 4)
    r0 = remote(tok.at[pl.ds(0, half)], chunk(x, c, 0, half), send.at[0], recv.at[0], right)
    r1 = remote(tok.at[pl.ds(half, half)], chunk(x, c, half, half), send.at[1], recv.at[1], right)
    l1 = remote(tok.at[pl.ds(half, half)], chunk(x, c, half, half), send.at[2], recv.at[2], left)
    l0 = remote(tok.at[pl.ds(0, half)], chunk(x, c, 0, half), send.at[3], recv.at[3], left)
    m0 = remote(tok, chunk(x, c), send.at[4], recv.at[4], mate)
    m0.start()
    r0.start()
    l1.start()
    r1.start()
    l0.start()
    loads = [
        pltpu.make_async_copy(wz, wzx_v.at[:, pl.ds(0, width)], local.at[1]),
        pltpu.make_async_copy(wx, wzx_v.at[:, pl.ds(width, width)], local.at[2]),
        pltpu.make_async_copy(wbc, wbc_v, local.at[3]),
    ]
    for load in loads:
        load.start()
    to_seg = remote(seg, seg_s, send.at[11], recv.at[11], after)
    to_seg.start()
    to_wo = remote(wo, wo_out, send.at[12], recv.at[12], mate)
    to_wo.start()
    r2 = remote(chunk(x - 1, c, 0, half), chunk(x - 1, c, 0, half), send.at[5], recv.at[5], right)
    l2 = remote(chunk(x + 1, c, half, half), chunk(x + 1, c, half, half), send.at[6], recv.at[6], left)
    m1 = remote(chunk(x - 1, c), chunk(x - 1, c), send.at[7], recv.at[7], mate)
    m2 = remote(chunk(x + 1, c), chunk(x + 1, c), send.at[8], recv.at[8], mate)
    m3 = remote(chunk(x + 2, c), chunk(x + 2, c), send.at[9], recv.at[9], mate)
    last = xbc_out.shape[0] - HALO
    to_halo = remote(xbc_out.at[pl.ds(last, HALO)], halo_s, send.at[10], recv.at[10], after)

    wdt_v[...] = jnp.zeros_like(wdt_v)
    wdt_v[pl.ds(0, wdt.shape[0]), :] = wdt[...]

    def step(s, carry):
        @pl.when(s == 0)
        def _():
            own.wait()
            for load in loads:
                load.wait()
            m0.wait_recv()

        @pl.when(s == 1)
        def _():
            r0.wait_recv()
            r2.start()
            l1.wait_recv()
            l2.start()
            r1.wait_recv()
            m1.start()
            l0.wait_recv()
            m2.start()
            m1.wait_recv()

        @pl.when(s == 2)
        def _():
            m2.wait_recv()

        @pl.when(s == 3)
        def _():
            r2.wait_recv()
            l2.wait_recv()
            m3.start()
            m3.wait_recv()

        offset = jnp.where(s == 1, nx - 1, jnp.where(s == 2, 1, jnp.where(s == 3, 2, 0)))
        g = lax.rem(x + offset, nx)
        mine = pl.ds(pl.multiple_of(g * 2 * rows, 2 * rows), 2 * rows)
        v = mm(buf[mine, :], wbc_v[...]).astype(BF16)
        xbc_out[mine, pl.ds(width, 256)] = v
        v = mm(buf[mine, :], wzx_v[:, pl.ds(512, 256)]).astype(BF16)
        xbc_out[mine, pl.ds(128, 256)] = v
        v = mm(buf[mine, :], wzx_v[:, pl.ds(256, 256)]).astype(BF16)
        z_out[mine, pl.ds(256, 128)] = v[:, :128]
        xbc_out[mine, pl.ds(0, 128)] = v[:, 128:]
        v = mm(buf[mine, :], wzx_v[:, pl.ds(0, 256)]).astype(BF16)
        z_out[mine, pl.ds(0, 256)] = v
        v = lax.dot_general(
            buf[mine, :], wdt_v[...], (((1,), (1,)), ((), ())), preferred_element_type=F32
        )
        dt_out[mine, :] = v.astype(BF16).astype(F32)

        @pl.when(g == nx - 1)
        def _():
            to_halo.start()

        return carry

    lax.fori_loop(0, 4, step, 0)
    to_seg.wait_recv()
    seg_out[...] = seg_s[...]
    to_halo.wait_recv()
    halo_out[...] = halo_s[...]
    to_wo.wait_recv()
    for copy in (r0, r1, l1, l0, m0, r2, l2, m1, m2, m3, to_halo, to_seg, to_wo):
        copy.wait_send()


def gather_project(nx, nt, tokens, seg, w_z, w_x, w_bc, w_dt, w_out):
    rows, depth = tokens.shape
    width = w_z.shape[1]
    total = rows * nx * 2
    wide = width + w_bc.shape[1]
    hbm = whole(pl.ANY)
    return pl.pallas_call(
        functools.partial(gather_kernel, nx, nt),
        out_shape=(
            jax.ShapeDtypeStruct((total, width), BF16),
            jax.ShapeDtypeStruct((total, wide), BF16),
            jax.ShapeDtypeStruct((total, LANES), F32),
            jax.ShapeDtypeStruct((HALO, wide), BF16),
            jax.ShapeDtypeStruct(seg.shape, jnp.int32),
            jax.ShapeDtypeStruct(w_out.shape, BF16),
        ),
        in_specs=[hbm, whole(), hbm, hbm, hbm, whole(), hbm],
        out_specs=(whole(), whole(), whole(), whole(), whole(), hbm),
        scratch_shapes=[
            pltpu.VMEM((total, depth), BF16),
            pltpu.VMEM((depth, 2 * width), BF16),
            pltpu.VMEM((depth, w_bc.shape[1]), BF16),
            pltpu.VMEM((LANES, depth), BF16),
            pltpu.VMEM((HALO, wide), BF16),
            pltpu.VMEM(seg.shape, jnp.int32),
            pltpu.SemaphoreType.DMA((13,)),
            pltpu.SemaphoreType.DMA((13,)),
            pltpu.SemaphoreType.DMA((4,)),
        ],
        compiler_params=pltpu.CompilerParams(
            collective_id=0, has_side_effects=True, vmem_limit_bytes=VMEM_LIMIT
        ),
        name="gather_project",
    )(tokens, seg, w_z, w_x, w_bc, w_dt.T, w_out)


def scan_kernel(
    nt, heads,
    z, xbc, dt, halo, seg_before, seg, conv_x, conv_bc, gain, bias, rate, skip,
    g_out, ss_out,
    xs_s, b_s, c_s, segc, logs_s, dts_s, fresh_s, keep_s, y_s, local_s, decay_s,
    out0, out1, out2, in0, in1, in2, send, recv,
):
    t, x, c = here()
    after = at(lax.rem(t + 1, nt), x, c)
    before = at(lax.rem(t + nt - 1, nt), x, c)
    block, width = z.shape
    count = block // GROUP
    tiles = width // LANES
    head_dim = width // heads
    per = LANES // head_dim
    lane = lax.broadcasted_iota(jnp.int32, (1, LANES), 1)
    outs, ins = (out0, out1, out2), (in0, in1, in2)
    hops = [remote(outs[k], ins[k], send.at[k], recv.at[k], after) for k in range(3)]

    def scalars(ref):
        row = jnp.zeros((1, LANES), F32)
        for h in range(heads):
            row = jnp.where(lane == h, ref[h], row)
        return row

    def spread(cols, p):
        out = cols[:, p * per : p * per + 1]
        for q in range(1, per):
            out = jnp.where(lane >= q * head_dim, cols[:, p * per + q : p * per + q + 1], out)
        return jnp.broadcast_to(out, (cols.shape[0], LANES))

    greet((before,), 1)

    def columns(row):
        return jnp.transpose(jnp.broadcast_to(row.astype(F32), (LANES, LANES)))

    old = columns(seg_before[pl.ds(seg_before.shape[0] - 1, 1), :])
    old = jnp.where(t == 0, -1.0, old)
    segc[pl.ds(0, HALO), :] = old[LANES - HALO :, :]
    for i in range(block // LANES):
        segc[pl.ds(HALO + i * LANES, LANES), :] = columns(seg[pl.ds(i, 1), :])

    bias_row, rate_row = scalars(bias), scalars(rate)
    ones_low = (
        lax.broadcasted_iota(jnp.int32, (GROUP, GROUP), 0)
        >= lax.broadcasted_iota(jnp.int32, (GROUP, GROUP), 1)
    ).astype(F32)

    def first(g, carry):
        base = pl.multiple_of(g * GROUP, GROUP)
        mine = pl.ds(base, GROUP)
        back = pl.ds(pl.multiple_of(jnp.maximum(base - HALO, 0), HALO), HALO)
        sfull = segc[pl.ds(pl.multiple_of(base + 8, 8), GROUP + 8), :]
        scur = sfull[8:, :]
        same = [(pltpu.roll(sfull, 3 - k, 0)[8:, :] == scur).astype(F32) for k in range(3)]
        for j in range(tiles + 2):
            cols = pl.ds(j * LANES, LANES)
            prev = jnp.where(g == 0, halo[:, cols].astype(F32), xbc[back, cols].astype(F32))
            cur = xbc[mine, cols].astype(F32)
            full = jnp.concatenate([prev[8:, :], cur], axis=0)
            if j < tiles:
                taps = conv_x[:, cols]
            else:
                taps = conv_bc[:, pl.ds((j - tiles) * LANES, LANES)]
            total = pltpu.roll(full, 3, 0)[8:, :] * taps[0:1, :] * same[0]
            total = total + pltpu.roll(full, 2, 0)[8:, :] * taps[1:2, :] * same[1]
            total = total + pltpu.roll(full, 1, 0)[8:, :] * taps[2:3, :] * same[2]
            total = total + cur * taps[3:4, :]
            val = (total * (1.0 / (1.0 + jnp.exp(-total)))).astype(BF16)
            if j < tiles:
                xs_s[mine, cols] = val
            elif j == tiles:
                b_s[mine, :] = val
            else:
                c_s[mine, :] = val
        raw = dt[mine, :] + bias_row
        dts = jnp.maximum(raw, 0.0) + jnp.log1p(jnp.exp(-jnp.abs(raw)))
        logs = jnp.dot(
            ones_low, -dts * rate_row, preferred_element_type=F32, precision=lax.Precision.HIGHEST
        )
        dts_s[mine, :] = dts
        logs_s[mine, :] = logs
        final = logs[GROUP - 1 :, :]
        seg_last = scur[GROUP - 1 :, :]
        seg_in = sfull[7:8, :]
        tail = jnp.exp(final - logs) * (scur == seg_last).astype(F32) * dts
        keep = jnp.exp(final) * (seg_last == seg_in).astype(F32)
        scaled, kept = [], []
        for p in range(tiles):
            xs = xs_s[mine, pl.ds(p * LANES, LANES)].astype(F32)
            scaled.append((xs * spread(tail, p)).astype(BF16))
            kept.append(jnp.broadcast_to(spread(keep, p), (8, LANES)))
        keep_wide = jnp.concatenate(kept, axis=1)
        keep_s[pl.ds(pl.multiple_of(g * 8, 8), 8), :] = keep_wide
        fresh = lax.dot_general(
            b_s[mine, :], jnp.concatenate(scaled, axis=1), (((0,), (0,)), ((), ())),
            preferred_element_type=F32,
        )
        fresh_s[g] = fresh

        @pl.when(g == 0)
        def _():
            local_s[...] = fresh
            decay_s[...] = keep_wide

        @pl.when(g > 0)
        def _():
            local_s[...] = local_s[...] * keep_wide[0:1, :] + fresh
            decay_s[...] = decay_s[...] * keep_wide

        return carry

    lax.fori_loop(0, count, first, 0)
    out0[...] = local_s[...].astype(BF16)

    skip_rows = []
    for p in range(tiles):
        row = jnp.full((1, LANES), skip[p * per], F32)
        for q in range(1, per):
            row = jnp.where(lane >= q * head_dim, skip[p * per + q], row)
        skip_rows.append(row)
    below = lax.broadcasted_iota(jnp.int32, (LANES, LANES), 0) >= lax.broadcasted_iota(
        jnp.int32, (LANES, LANES), 1
    )

    def mix(g):
        base = pl.multiple_of(g * GROUP, GROUP)
        mine = pl.ds(base, GROUP)
        scur = segc[pl.ds(base + HALO, GROUP), :]
        srow = [seg[pl.ds(g * 2 + i, 1), :].astype(F32) for i in range(2)]
        scores = lax.dot_general(
            c_s[mine, :], b_s[mine, :], (((1,), (1,)), ((), ())), preferred_element_type=F32
        )
        lo, hi = slice(0, LANES), slice(LANES, GROUP)
        s00 = jnp.where(below & (scur[lo] == srow[0]), scores[lo, lo], 0.0)
        s10 = jnp.where(scur[hi] == srow[0], scores[hi, lo], 0.0)
        s11 = jnp.where(below & (scur[hi] == srow[1]), scores[hi, hi], 0.0)
        logs = logs_s[mine, :]
        lrow = jnp.transpose(logs)[0:8, :]
        drow = jnp.transpose(dts_s[mine, :])[0:8, :]
        for p in range(tiles):
            cols = pl.ds(p * LANES, LANES)
            xs = xs_s[mine, cols]
            total = None
            for q in range(per):
                h = p * per + q
                lc = logs[:, h : h + 1]
                lr, dr = lrow[h : h + 1, :], drow[h : h + 1, :]

                def piece(s, i, j):
                    return (s * jnp.exp(jnp.minimum(lc[i] - lr[:, j], 0.0)) * dr[:, j]).astype(BF16)

                top = jnp.concatenate([piece(s00, lo, lo), jnp.zeros((LANES, LANES), BF16)], axis=1)
                low = jnp.concatenate([piece(s10, hi, lo), piece(s11, hi, hi)], axis=1)
                part = (lane >= q * head_dim) & (lane < (q + 1) * head_dim)
                term = mm(
                    jnp.concatenate([top, low], axis=0), jnp.where(part, xs, jnp.zeros_like(xs))
                )
                total = term if total is None else total + term
            y_s[mine, cols] = total + skip_rows[p] * xs.astype(F32)

    mix(0)
    hops[0].start()
    mix(1)
    hops[0].wait_recv()
    decay = decay_s[0:1, :]
    out1[...] = (local_s[...] + decay * in0[...].astype(F32)).astype(BF16)
    hops[1].start()
    mix(2)
    hops[1].wait_recv()
    out2[...] = (local_s[...] + decay * in1[...].astype(F32)).astype(BF16)
    hops[2].start()
    mix(3)
    hops[2].wait_recv()
    local_s[...] = in2[...].astype(F32)
    eye = (
        lax.broadcasted_iota(jnp.int32, (LANES, LANES), 0)
        == lax.broadcasted_iota(jnp.int32, (LANES, LANES), 1)
    )

    def second(g, carry):
        base = pl.multiple_of(g * GROUP, GROUP)
        mine = pl.ds(base, GROUP)
        ssm = local_s[...]
        high = ssm.astype(BF16)
        low = (ssm - high.astype(F32)).astype(BF16)
        cm = c_s[mine, :]
        carried = mm(cm, high) + mm(cm, low)
        sfull = segc[pl.ds(pl.multiple_of(base + 8, 8), GROUP + 8), :]
        enter = jnp.exp(logs_s[mine, :]) * (sfull[8:, :] == sfull[7:8, :]).astype(F32)
        squares = jnp.zeros((GROUP, LANES), F32)
        for p in range(tiles):
            cols = pl.ds(p * LANES, LANES)
            zz = z[mine, cols].astype(F32)
            val = y_s[mine, cols] + carried[:, p * LANES : (p + 1) * LANES] * spread(enter, p)
            val = val * (zz * (1.0 / (1.0 + jnp.exp(-zz))))
            squares = squares + val * val
            g_out[mine, cols] = (val * gain[:, cols]).astype(BF16)
        sums = jnp.sum(squares, axis=1, keepdims=True)
        for i in range(GROUP // LANES):
            row = jnp.sum(jnp.where(eye, sums[i * LANES : (i + 1) * LANES, :], 0.0), axis=0, keepdims=True)
            ss_out[g * (GROUP // LANES) + i] = jnp.broadcast_to(row, (8, LANES))
        local_s[...] = ssm * keep_s[pl.ds(pl.multiple_of(g * 8, 8), 8), :][0:1, :] + fresh_s[g]
        return carry

    lax.fori_loop(0, count, second, 0)
    for hop in hops:
        hop.wait_send()


def scan(nt, z, xbc, dt, halo, seg_before, seg, conv_x, conv_bc, gain, bias, rate, skip):
    block, width = z.shape
    heads = rate.shape[0]
    count = block // GROUP
    state = LANES
    smem = whole(pltpu.SMEM)
    return pl.pallas_call(
        functools.partial(scan_kernel, nt, heads),
        out_shape=(
            jax.ShapeDtypeStruct((block, width), BF16),
            jax.ShapeDtypeStruct((block // LANES, 8, LANES), F32),
        ),
        in_specs=[whole()] * 9 + [smem] * 3,
        out_specs=(whole(), whole()),
        scratch_shapes=[
            pltpu.VMEM((block, width), BF16),
            pltpu.VMEM((block, state), BF16),
            pltpu.VMEM((block, state), BF16),
            pltpu.VMEM((block + HALO, LANES), F32),
            pltpu.VMEM((block, LANES), F32),
            pltpu.VMEM((block, LANES), F32),
            pltpu.VMEM((count, state, width), F32),
            pltpu.VMEM((count * 8, width), F32),
            pltpu.VMEM((block, width), F32),
            pltpu.VMEM((state, width), F32),
            pltpu.VMEM((8, width), F32),
        ]
        + [pltpu.VMEM((state, width), BF16)] * 6
        + [pltpu.SemaphoreType.DMA((3,)), pltpu.SemaphoreType.DMA((3,))],
        compiler_params=pltpu.CompilerParams(
            collective_id=1, has_side_effects=True, vmem_limit_bytes=VMEM_LIMIT
        ),
        name="scan_block",
    )(z, xbc, dt, halo, seg_before, seg, conv_x, conv_bc, gain, bias, rate, skip)


def scatter_kernel(
    nx, total_width, g_in, ss, wo, wo_mate, out,
    wo_v, g2, to_r, to_l, far_r, far_l, near_r, near_l, from_l, from_r, keep_r, keep_l, acc, ss_in,
    send, recv, local,
):
    t, x, c = here()
    n = 2 * nx
    w = x * 2 + c
    rows, cols = out.shape
    half = rows // 2
    width = g_in.shape[1]
    right = at(t, lax.rem(x + 1, nx), c)
    left = at(t, lax.rem(x + nx - 1, nx), c)
    mate = at(t, x, 1 - c)

    def rot(k):
        return lax.rem(x + k, nx)

    loads = [
        pltpu.make_async_copy(wo, wo_v.at[pl.ds(0, width)], local.at[0]),
        pltpu.make_async_copy(wo_mate, wo_v.at[pl.ds(width, width)], local.at[1]),
    ]
    order = (2, 1, nx - 1, 0)
    swaps = []
    for i, k in enumerate(order):
        xx = rot(k)
        to = pl.ds(pl.multiple_of(xx * rows, rows), rows)
        src = g_in.at[pl.ds(pl.multiple_of((xx * 2 + c) * rows, rows), rows)]
        loads.append(pltpu.make_async_copy(src, g2.at[to, pl.ds(0, width)], local.at[2 + i]))
        src = g_in.at[pl.ds(pl.multiple_of((xx * 2 + 1 - c) * rows, rows), rows)]
        swaps.append(remote(src, g2.at[to, pl.ds(width, width)], send.at[i], recv.at[i], mate))
    for load in loads:
        load.start()
    others = [
        {"tm": t, "weight": lax.rem(w + k, n)} for k in range(1, n)
    ]
    greet(others, n - 1)
    for swap in swaps:
        swap.start()
    sums = []
    for k in range(1, n):
        dest = lax.rem(w + k, n)
        sums.append(remote(ss.at[dest], ss_in.at[w], send.at[9 + k], recv.at[9 + k], others[k - 1]))
    for copy in sums:
        copy.start()
    r0 = remote(to_r, far_r, send.at[4], recv.at[4], right)
    l0 = remote(to_l, far_l, send.at[5], recv.at[5], left)
    r1 = remote(near_r.at[1], from_l.at[1], send.at[6], recv.at[6], right)
    l1 = remote(near_l.at[0], from_r.at[0], send.at[7], recv.at[7], left)
    r2 = remote(near_r.at[0], from_l.at[0], send.at[8], recv.at[8], right)
    l2 = remote(near_l.at[1], from_r.at[1], send.at[9], recv.at[9], left)
    for load in loads:
        load.wait()

    piece = 256
    spans = [pl.ds(i * piece, piece) for i in range(cols // piece)]

    def product(k, span):
        own = pl.ds(pl.multiple_of(rot(k) * rows, rows), rows)
        return mm(g2[own, :], wo_v[:, span])

    swaps[0].wait_recv()
    for span in spans:
        v = product(2, span).astype(BF16)
        to_r[:, span] = v[:half]
        to_l[:, span] = v[half:]
    r0.start()
    l0.start()
    swaps[1].wait_recv()
    for span in spans:
        v = product(1, span)
        keep_r[:, span] = v[:half]
        near_r[1, :, span] = v[half:].astype(BF16)
    r1.start()
    swaps[2].wait_recv()
    for span in spans:
        v = product(nx - 1, span)
        near_l[0, :, span] = v[:half].astype(BF16)
        keep_l[:, span] = v[half:]
    l1.start()
    swaps[3].wait_recv()
    for span in spans:
        acc[:, span] = product(0, span)
    r0.wait_recv()
    for span in spans:
        near_r[0, :, span] = (keep_r[:, span] + far_r[:, span].astype(F32)).astype(BF16)
    r2.start()
    l0.wait_recv()
    for span in spans:
        near_l[1, :, span] = (keep_l[:, span] + far_l[:, span].astype(F32)).astype(BF16)
    l2.start()
    for copy in sums:
        copy.wait_recv()
    ss_in[w] = ss[w]
    square = jnp.sum(ss_in[...], axis=0)[0:1, :]
    inverse = lax.rsqrt(square / total_width + EPS)
    eye = (
        lax.broadcasted_iota(jnp.int32, (rows, rows), 0)
        == lax.broadcasted_iota(jnp.int32, (rows, rows), 1)
    )
    scale = jnp.sum(jnp.where(eye, inverse, 0.0), axis=1, keepdims=True)
    r1.wait_recv()
    l1.wait_recv()
    for span in spans:
        acc[pl.ds(half, half), span] = acc[pl.ds(half, half), span] + from_l[1, :, span].astype(F32)
        acc[pl.ds(0, half), span] = acc[pl.ds(0, half), span] + from_r[0, :, span].astype(F32)
    r2.wait_recv()
    l2.wait_recv()
    for span in spans:
        v = acc[pl.ds(0, half), span] + from_l[0, :, span].astype(F32)
        out[pl.ds(0, half), span] = (v * scale[:half]).astype(BF16)
        v = acc[pl.ds(half, half), span] + from_r[1, :, span].astype(F32)
        out[pl.ds(half, half), span] = (v * scale[half:]).astype(BF16)
    for copy in swaps + sums + [r0, l0, r1, l1, r2, l2]:
        copy.wait_send()


def project_scatter(nx, g, ss, w_out, w_mate):
    block, width = g.shape
    n = 2 * nx
    rows = block // n
    half = rows // 2
    cols = w_out.shape[1]
    hbm = whole(pl.ANY)
    return pl.pallas_call(
        functools.partial(scatter_kernel, nx, width * n),
        out_shape=jax.ShapeDtypeStruct((rows, cols), BF16),
        in_specs=[hbm, whole(), hbm, hbm],
        out_specs=whole(),
        scratch_shapes=[
            pltpu.VMEM((2 * width, cols), BF16),
            pltpu.VMEM((nx * rows, 2 * width), BF16),
            pltpu.VMEM((half, cols), BF16),
            pltpu.VMEM((half, cols), BF16),
            pltpu.VMEM((half, cols), BF16),
            pltpu.VMEM((half, cols), BF16),
            pltpu.VMEM((2, half, cols), BF16),
            pltpu.VMEM((2, half, cols), BF16),
            pltpu.VMEM((2, half, cols), BF16),
            pltpu.VMEM((2, half, cols), BF16),
            pltpu.VMEM((half, cols), F32),
            pltpu.VMEM((half, cols), F32),
            pltpu.VMEM((rows, cols), F32),
            pltpu.VMEM((n, 8, LANES), F32),
            pltpu.SemaphoreType.DMA((9 + n,)),
            pltpu.SemaphoreType.DMA((9 + n,)),
            pltpu.SemaphoreType.DMA((6,)),
        ],
        compiler_params=pltpu.CompilerParams(
            collective_id=2, has_side_effects=True, vmem_limit_bytes=VMEM_LIMIT
        ),
        name="project_scatter",
    )(g, ss, w_out, w_mate)


def on_device(
    tokens, segments, w_z, w_x, w_dt, w_bc, conv_x, conv_bc, dt_bias, decay_rate, skip_d,
    norm_gain, w_out,
):
    nx = lax.axis_size("weight") // 2
    nt = lax.axis_size("tm")
    seg = segments.reshape(-1, LANES)
    gain = norm_gain.astype(F32).reshape(1, -1)
    z, xbc, dt, halo, seg_before, w_mate = gather_project(
        nx, nt, tokens, seg, w_z, w_x, w_bc, w_dt, w_out
    )
    g, ss = scan(
        nt, z, xbc, dt, halo, seg_before, seg, conv_x, conv_bc, gain, dt_bias, decay_rate, skip_d
    )
    return project_scatter(nx, g, ss, w_out, w_mate)


def solution(mesh):
    return jax.shard_map(
        on_device,
        mesh=mesh,
        in_specs=(
            P(("tm", "weight"), None),
            P("tm"),
            P(None, "weight"),
            P(None, "weight"),
            P(None, "weight"),
            P(),
            P(None, "weight"),
            P(),
            P("weight"),
            P("weight"),
            P("weight"),
            P("weight"),
            P("weight", None),
        ),
        out_specs=P(("tm", "weight"), None),
        check_vma=False,
    )
```

time: 353 us -> 101 us (0.29)
  the two profiles are of different devices: /device:TPU:25 before, /device:TPU:64 now
where the time goes in v1:
time: 101 us
  Pallas kernels  97.5 us (97%)
  local copies, waits for them, and re-layouts  3.21 us (3%)
    pallas_call x1, Pallas kernels, project_scatter(): pl.pallas_call(functools.partial(scatter_kernel, nx, width * n), out_shap...  37.5 us
    pallas_call x1, Pallas kernels, gather_project(): pl.pallas_call(functools.partial(gather_kernel, nx, nt), out_shape=(jax.S...  32.4 us
    pallas_call x1, Pallas kernels, scan(): pl.pallas_call(functools.partial(scan_kernel, nt, heads), out_shape=(jax....  27.6 us

profile of v1, /device:TPU:64, one launch (start us, length us, event | category | flops | bytes accessed | tf_op | source)
XLA Modules:
  0.0 100.7 jit_solution(2694754330414228527)
XLA Ops:
  0.0 1.2 %reshape.12.gain = f32[1,384]{1,0:T(1,128)} reshape(bf16[384]{0:T(512)(128)(2,1)} %param.24) | data formatting | bytes 2304 | tf_op jit(solution)/shard_map/reshape | solution.py:612
  1.2 32.4 %gather_project.1 = (bf16[1024,384]{1,0:T(8,128)(2,1)}, bf16[1024,640]{1,0:T(8,128)(2,1)}, f32[1024,128]{1,0:T(8,128)}, bf16[16,640]{1,0:T(8,128)(2,1)}, s32[8,128]{1,0:T(8,128)}, /*index=5*/bf16[384,2560]{1,0:T(8,128)(2,1)}) custom-call(bf16[128,2560]{1,0:T(8,128)(2,1)} %tok.1, s32[8,128]{1,0:T(8,128)} %bitcast.3, bf16[2560,384]{1,0:T(8,128)(2,1)} %wz.1, ...), custom_call_target="tpu_custom_call" | custom-call | tf_op jit(solution)/shard_map/gather_project/pallas_call | solution.py:174
  33.6 27.6 %scan_block.1 = (bf16[1024,384]{1,0:T(8,128)(2,1)}, f32[8,8,128]{2,1,0:T(8,128)}) custom-call(bf16[1024,384]{1,0:T(8,128)(2,1)} %get-tuple-element.13.z, bf16[1024,640]{1,0:T(8,128)(2,1)} %get-tuple-element.14.xbc, f32[1024,128]{1,0:T(8,128)} %get-tuple-element.15.dt, bf16[16,640]{1,0:T(8,128)(2,1)} %get-tuple-element.16.halo, ...), custom_call_target="tpu_custom_call" | custom-call | tf_op jit(solution)/shard_map/scan_block/pallas_call | solution.py:420
  61.3 37.5 %project_scatter.1 = bf16[128,2560]{1,0:T(8,128)(2,1)} custom-call(bf16[1024,384]{1,0:T(8,128)(2,1)} %get-tuple-element.18.g_in, f32[8,8,128]{2,1,0:T(8,128)} %get-tuple-element.19.ss, bf16[384,2560]{1,0:T(8,128)(2,1)} %wo.3, bf16[384,2560]{1,0:T(8,128)(2,1)} %get-tuple-element.20.wo_mate), custom_call_target="tpu_custom_call" | custom-call | tf_op jit(solution)/shard_map/project_scatter/pallas_call | solution.py:574
  98.7 2.0 %copy.15 = bf16[128,2560]{1,0:T(8,128)(2,1)} copy(bf16[128,2560]{1,0:T(8,128)(2,1)} %project_scatter.1) | data formatting | bytes 1310720

commit v2 on v0

v2 whole, which is shorter than its diff:
```python
import functools

import jax
import jax.numpy as jnp
from jax import lax
from jax.experimental import pallas as pl
from jax.experimental.pallas import tpu as pltpu
from jax.sharding import PartitionSpec as P

GROUP = 256
LANES = 128
HALO = 16
HOPS = 3
PIECE = 256
EPS = 1e-5
F32 = jnp.float32
BF16 = jnp.bfloat16
MESH = pl.DeviceIdType.MESH
VMEM_LIMIT = 56 * 1024 * 1024
COPIES = 64


def whole(space=pltpu.VMEM):
    return pl.BlockSpec(memory_space=space)


def mm(a, b):
    return jnp.dot(a, b, preferred_element_type=F32)


def silu(v):
    h = 0.5 * v
    return h + h * jnp.tanh(h)


def layer_kernel(
    nx, nt, heads,
    tok, seg, wz, wx, wbc, wdt, conv_x, conv_bc, gain, wo, bias, rate, skip,
    out,
    buf, wa_v, wz_v, wd_f, wo_v, z_s, xbc_s, dt_s, halo_s, seg_s,
    segc, mask_s, cv_s, cvh_s, xs_s, b_s, c_s, logs_s, dts_s, fresh_s, keep_s, y_s, ex_s, local_s, decay_s,
    ssm_s, kcum_s, hop_out, hop_in, enter_s, g_s, ss_s, ss_in,
    to_r, to_l, far_r, far_l, near_r, near_l, from_l, from_r, keep_r, keep_l, acc,
    send, recv, local,
):
    t = lax.axis_index("tm")
    w = lax.axis_index("weight")
    x, c = lax.div(w, 2), lax.rem(w, 2)
    n = 2 * nx
    rows, depth = tok.shape
    half, quarter = rows // 2, rows // 4
    width = wz.shape[1]
    block = rows * n
    tiles = width // LANES
    head_dim = width // heads
    per = LANES // head_dim
    lane = lax.broadcasted_iota(jnp.int32, (1, LANES), 1)

    def at(tt, xx, cc):
        return {"tm": tt, "weight": xx * 2 + cc}

    def rot(k):
        return lax.rem(x + (k + nx) % nx, nx)

    right, left, mate = at(t, rot(1), c), at(t, rot(-1), c), at(t, x, 1 - c)
    after = at(lax.rem(t + 1, nt), x, c)
    before = at(lax.rem(t + nt - 1, nt), x, c)
    copies = []

    def remote(src, dst, device):
        k = len(copies)
        copy = pltpu.make_async_remote_copy(
            src_ref=src, dst_ref=dst, send_sem=send.at[k], recv_sem=recv.at[k],
            device_id=device, device_id_type=MESH,
        )
        copies.append(copy)
        return copy

    def chunk(xx, start=0, size=rows):
        begin = (xx * 2 + c) * rows + start
        return buf.at[pl.ds(pl.multiple_of(begin, quarter), size)]

    def same_place(xx, start, size, device):
        return remote(chunk(xx, start, size), chunk(xx, start, size), device)

    own = pltpu.make_async_copy(tok, chunk(x), local.at[0])
    own.start()
    loads = [
        pltpu.make_async_copy(wx, wa_v.at[:, pl.ds(0, width)], local.at[1]),
        pltpu.make_async_copy(wbc, wa_v.at[:, pl.ds(width, wbc.shape[1])], local.at[2]),
        pltpu.make_async_copy(wz, wz_v, local.at[3]),
    ]
    for load in loads:
        load.start()
    load_wo = pltpu.make_async_copy(wo, wo_v.at[pl.ds(0, width)], local.at[4])
    load_wo.start()
    others = [{"tm": t, "weight": lax.rem(w + k, n)} for k in range(1, n)]
    barrier = pltpu.get_barrier_semaphore()
    for device in others + [before]:
        pl.semaphore_signal(barrier, inc=1, device_id=device, device_id_type=MESH)
    pl.semaphore_wait(barrier, n)

    xl, xr, xf = rot(-1), rot(1), rot(2)
    lo_half, hi_half = pl.ds(0, half), pl.ds(half, half)
    m0 = remote(tok, chunk(x), mate)
    a_r0 = remote(tok.at[lo_half], chunk(x, 0, half), right)
    a_l1 = remote(tok.at[hi_half], chunk(x, half, half), left)
    a_r1 = remote(tok.at[hi_half], chunk(x, half, half), right)
    a_l0 = remote(tok.at[lo_half], chunk(x, 0, half), left)
    to_seg = remote(seg, seg_s, after)
    for copy in (m0, a_r0, a_l1, a_r1, a_l0, to_seg):
        copy.start()
    to_wo = remote(wo, wo_v.at[pl.ds(width, width)], mate)
    to_wo.start()
    relay_r = [same_place(xl, q * quarter, quarter, right) for q in (0, 1)]
    relay_l = [same_place(xr, half + q * quarter, quarter, left) for q in (0, 1)]
    fwd_l0, fwd_l1 = same_place(xl, 0, half, mate), same_place(xl, half, half, mate)
    fwd_r1, fwd_r0 = same_place(xr, half, half, mate), same_place(xr, 0, half, mate)
    fwd_f = [
        [same_place(xf, q * quarter, quarter, mate), same_place(xf, half + q * quarter, quarter, mate)]
        for q in (0, 1)
    ]
    to_halo = remote(xbc_s.at[pl.ds(block - HALO, HALO)], halo_s, after)

    wd_f[...] = jnp.zeros_like(wd_f)
    wd_f[pl.ds(0, heads), :] = wdt[...].astype(F32)
    for i in range(depth // LANES):
        cols = pl.ds(i * LANES, LANES)
        part = jnp.concatenate([wd_f[:, cols], jnp.zeros((LANES - 8, LANES), F32)], axis=0)
        wa_v[cols, pl.ds(width + 2 * LANES, LANES)] = jnp.transpose(part).astype(BF16)

    def columns(row):
        return jnp.transpose(jnp.broadcast_to(row.astype(F32), (LANES, LANES)))

    def scalars(ref):
        row = jnp.zeros((1, LANES), F32)
        for h in range(heads):
            row = jnp.where(lane == h, ref[h], row)
        return row

    def spread(cols, p):
        value = cols[:, p * per : p * per + 1]
        for q in range(1, per):
            value = jnp.where(lane >= q * head_dim, cols[:, p * per + q : p * per + q + 1], value)
        return jnp.broadcast_to(value, (cols.shape[0], LANES))

    for i in range(block // LANES):
        segc[pl.ds(HALO + i * LANES, LANES), :] = columns(seg[pl.ds(i, 1), :])
    bias_row, rate_row = scalars(bias), scalars(rate)
    skip_rows = []
    for p in range(tiles):
        row = jnp.full((1, LANES), skip[p * per], F32)
        for q in range(1, per):
            row = jnp.where(lane >= q * head_dim, skip[p * per + q], row)
        skip_rows.append(row)

    to_seg.wait_recv()
    old = columns(seg_s[pl.ds(seg_s.shape[0] - 1, 1), :])
    old = jnp.where(t == 0, -1.0, old)
    segc[pl.ds(0, HALO), :] = old[LANES - HALO :, :]
    for k in range(3):
        for i in range(block // LANES):
            now = segc[pl.ds(HALO + i * LANES, LANES), :]
            then = segc[pl.ds(HALO + i * LANES - 3 + k, LANES), :]
            mask_s[k, pl.ds(i * LANES, LANES), :] = (now == then).astype(F32)

    def span(g, start=0, size=GROUP):
        return pl.ds(pl.multiple_of(g * GROUP + start, HALO), size)

    def project_xbc(g):
        mine = span(g)
        v = mm(buf[mine, :], wa_v[:, pl.ds(0, 256)]).astype(BF16)
        xbc_s[mine, pl.ds(0, 256)] = v
        v = mm(buf[mine, :], wa_v[:, pl.ds(256, 256)]).astype(BF16)
        xbc_s[mine, pl.ds(256, 256)] = v
        v = mm(buf[mine, :], wa_v[:, pl.ds(512, 256)]).astype(BF16)
        xbc_s[mine, pl.ds(512, 128)] = v[:, :128]
        dt_s[mine, :] = v[:, 128:].astype(F32)

    def halo_if_last(g):
        @pl.when(g == nx - 1)
        def _():
            to_halo.start()

    def project_z(g):
        mine = span(g)
        z_s[mine, pl.ds(0, 256)] = mm(buf[mine, :], wz_v[:, pl.ds(0, 256)]).astype(BF16)
        z_s[mine, pl.ds(256, 128)] = mm(buf[mine, :], wz_v[:, pl.ds(256, 128)]).astype(BF16)

    def taps_of(j):
        if j < tiles:
            return conv_x[:, pl.ds(j * LANES, LANES)]
        return conv_bc[:, pl.ds((j - tiles) * LANES, LANES)]

    def conv_store(j, where, val):
        if j < tiles:
            xs_s[where, pl.ds(j * LANES, LANES)] = val
        elif j == tiles:
            b_s[where, :] = val
        else:
            c_s[where, :] = val

    def conv_rows(j, source, g, start, size):
        taps = taps_of(j)
        mine = span(g, start, size)
        total = source[pl.ds(HALO - 3, size), :] * taps[0:1, :] * mask_s[0, mine, :]
        total = total + source[pl.ds(HALO - 2, size), :] * taps[1:2, :] * mask_s[1, mine, :]
        total = total + source[pl.ds(HALO - 1, size), :] * taps[2:3, :] * mask_s[2, mine, :]
        total = total + source[pl.ds(HALO, size), :] * taps[3:4, :]
        conv_store(j, mine, silu(total).astype(BF16))

    def conv_main(g):
        for j in range(tiles + 2):
            cv_s[j] = xbc_s[span(g), pl.ds(j * LANES, LANES)].astype(F32)
            conv_rows(j, cv_s.at[j], g, HALO, GROUP - HALO)

    def conv_head(g):
        for j in range(tiles + 2):
            cols = pl.ds(j * LANES, LANES)
            back = pl.ds(pl.multiple_of(jnp.maximum(g * GROUP - HALO, 0), HALO), HALO)

            @pl.when(g == 0)
            def _():
                cvh_s[j, pl.ds(0, HALO), :] = halo_s[:, cols].astype(F32)

            @pl.when(g > 0)
            def _():
                cvh_s[j, pl.ds(0, HALO), :] = xbc_s[back, cols].astype(F32)

            cvh_s[j, pl.ds(HALO, HALO), :] = xbc_s[span(g, 0, HALO), cols].astype(F32)
        for j in range(tiles + 2):
            conv_rows(j, cvh_s.at[j], g, 0, HALO)

    low_ones = (
        lax.broadcasted_iota(jnp.int32, (GROUP, GROUP), 0)
        >= lax.broadcasted_iota(jnp.int32, (GROUP, GROUP), 1)
    ).astype(F32).astype(BF16)

    def steps(g):
        mine = span(g)
        raw = dt_s[mine, :] + bias_row
        dts = jnp.maximum(raw, 0.0) + jnp.log1p(jnp.exp(-jnp.abs(raw)))
        rest = -dts * rate_row
        logs = jnp.zeros((GROUP, LANES), F32)
        for _ in range(3):
            part = rest.astype(BF16)
            rest = rest - part.astype(F32)
            logs = logs + mm(low_ones, part)
        dts_s[mine, :] = dts
        logs_s[mine, :] = logs

    def documents(g):
        base = g * GROUP
        cur = segc[pl.ds(pl.multiple_of(base + HALO, 8), GROUP), :]
        return cur, segc[pl.ds(pl.multiple_of(base + HALO - 8, 8), 8), :][7:8, :]

    def state(g):
        mine = span(g)
        logs, dts = logs_s[mine, :], dts_s[mine, :]
        cur, seg_in = documents(g)
        seg_last = cur[GROUP - 1 :, :]
        final = logs[GROUP - 1 :, :]
        tail = jnp.exp(final - logs) * (cur == seg_last).astype(F32) * dts
        keep = jnp.exp(final) * (seg_last == seg_in).astype(F32)
        scaled, kept = [], []
        for p in range(tiles):
            xs = xs_s[mine, pl.ds(p * LANES, LANES)].astype(F32)
            scaled.append((xs * spread(tail, p)).astype(BF16))
            kept.append(jnp.broadcast_to(spread(keep, p), (8, LANES)))
        keep_s[g] = jnp.concatenate(kept, axis=1)
        fresh_s[g] = lax.dot_general(
            b_s[mine, :], jnp.concatenate(scaled, axis=1), (((0,), (0,)), ((), ())),
            preferred_element_type=F32,
        )

    below = lax.broadcasted_iota(jnp.int32, (LANES, LANES), 0) >= lax.broadcasted_iota(
        jnp.int32, (LANES, LANES), 1
    )
    lo, hi = slice(0, LANES), slice(LANES, GROUP)

    def mix(g):
        mine = span(g)
        cur, seg_in = documents(g)
        srow = [seg[pl.ds(g * 2 + i, 1), :].astype(F32) for i in range(2)]
        scores = lax.dot_general(
            c_s[mine, :], b_s[mine, :], (((1,), (1,)), ((), ())), preferred_element_type=F32
        )
        s00 = jnp.where(below & (cur[lo] == srow[0]), scores[lo, lo], 0.0)
        s10 = jnp.where(cur[hi] == srow[0], scores[hi, lo], 0.0)
        s11 = jnp.where(below & (cur[hi] == srow[1]), scores[hi, hi], 0.0)
        logs = logs_s[mine, :]
        lrow = jnp.transpose(logs)[0:8, :]
        drow = jnp.transpose(dts_s[mine, :])[0:8, :]
        ssm = ssm_s[...]
        high = ssm.astype(BF16)
        low = (ssm - high.astype(F32)).astype(BF16)
        cm = c_s[mine, :]
        carried = mm(cm, high) + mm(cm, low)
        enter = jnp.exp(logs) * (cur == seg_in).astype(F32)
        for p in range(tiles):
            cols = pl.ds(p * LANES, LANES)
            xs = xs_s[mine, cols]
            total = None
            for q in range(per):
                h = p * per + q
                lc = logs[:, h : h + 1]
                lr, dr = lrow[h : h + 1, :], drow[h : h + 1, :]

                def piece(s, i, j):
                    return (s * jnp.exp(jnp.minimum(lc[i] - lr[:, j], 0.0)) * dr[:, j]).astype(BF16)

                top = jnp.concatenate([piece(s00, lo, lo), jnp.zeros((LANES, LANES), BF16)], axis=1)
                bot = jnp.concatenate([piece(s10, hi, lo), piece(s11, hi, hi)], axis=1)
                part = (lane >= q * head_dim) & (lane < (q + 1) * head_dim)
                term = mm(
                    jnp.concatenate([top, bot], axis=0), jnp.where(part, xs, jnp.zeros_like(xs))
                )
                total = term if total is None else total + term
            wide = spread(enter, p)
            gate = silu(z_s[mine, cols].astype(F32))
            inside = total + carried[:, p * LANES : (p + 1) * LANES] * wide
            y_s[mine, cols] = (inside + skip_rows[p] * xs.astype(F32)) * gate
            ex_s[mine, cols] = wide * kcum_s[0:1, cols] * gate
        kept = keep_s[g]
        ssm_s[...] = ssm * kept[0:1, :] + fresh_s[g]
        kcum_s[...] = kcum_s[...] * kept

    for load in loads:
        load.wait()
    own.wait()
    m0.wait_recv()
    project_xbc(x)
    halo_if_last(x)
    project_z(x)
    conv_main(x)
    steps(x)
    a_r0.wait_recv()
    a_l1.wait_recv()
    for copy in relay_r + relay_l + [fwd_l0, fwd_r1]:
        copy.start()
    a_r1.wait_recv()
    fwd_l1.start()
    a_l0.wait_recv()
    fwd_r0.start()
    fwd_l0.wait_recv()
    fwd_l1.wait_recv()
    project_xbc(xl)
    halo_if_last(xl)
    fwd_r1.wait_recv()
    fwd_r0.wait_recv()
    project_xbc(xr)
    halo_if_last(xr)
    relay_r[0].wait_recv()
    fwd_f[0][0].start()
    relay_l[0].wait_recv()
    fwd_f[0][1].start()
    conv_main(xl)
    steps(xl)
    conv_main(xr)
    steps(xr)

    def halo_wait(places):
        @pl.when(places)
        def _():
            to_halo.wait_recv()

    halo_wait((x == 0) | (x == nx - 1))

    conv_head(xr)
    relay_r[1].wait_recv()
    fwd_f[1][0].start()
    relay_l[1].wait_recv()
    fwd_f[1][1].start()
    state(xr)
    conv_head(x)
    state(x)
    project_z(xl)
    for pair in fwd_f:
        for copy in pair:
            copy.wait_recv()
    project_xbc(xf)
    halo_if_last(xf)
    conv_main(xf)
    steps(xf)
    halo_wait(x == 2)
    conv_head(xf)
    state(xf)
    halo_wait(x == 1)
    conv_head(xl)
    state(xl)

    hops = [
        [remote(hop_out.at[h, p], hop_in.at[h, p], after) for p in range(tiles)]
        for h in range(HOPS)
    ]
    for p in range(tiles):
        cols = pl.ds(p * LANES, LANES)
        total, decay = fresh_s[0, :, cols], keep_s[0, :, cols]
        for g in range(1, nx):
            total = total * keep_s[g, 0:1, cols] + fresh_s[g, :, cols]
            decay = decay * keep_s[g, :, cols]
        local_s[:, cols] = total
        decay_s[:, cols] = decay
        hop_out[0, p] = total.astype(BF16)
        hops[0][p].start()

    def hop_on(h):
        for p in range(tiles):
            cols = pl.ds(p * LANES, LANES)
            hops[h - 1][p].wait_recv()
            total = local_s[:, cols] + decay_s[0:1, cols] * hop_in[h - 1, p].astype(F32)
            hop_out[h, p] = total.astype(BF16)
            hops[h][p].start()

    ssm_s[...] = jnp.zeros_like(ssm_s)
    kcum_s[...] = jnp.ones_like(kcum_s)

    def mix_step(g, carry):
        mix(g)
        return carry

    project_z(xr)
    project_z(xf)
    lax.fori_loop(0, 1, mix_step, 0)
    hop_on(1)
    lax.fori_loop(1, 3, mix_step, 0)
    hop_on(2)
    lax.fori_loop(3, nx, mix_step, 0)
    load_wo.wait()
    to_wo.wait_recv()
    for p in range(tiles):
        hops[HOPS - 1][p].wait_recv()
        enter_s[:, pl.ds(p * LANES, LANES)] = hop_in[HOPS - 1, p]

    eye = (
        lax.broadcasted_iota(jnp.int32, (LANES, LANES), 0)
        == lax.broadcasted_iota(jnp.int32, (LANES, LANES), 1)
    )
    order = (2, 1, -1, 0)
    swaps = []
    for k in order:
        to = pl.ds(pl.multiple_of(rot(k) * rows, rows), rows)
        swaps.append(
            remote(g_s.at[1, to, pl.ds(0, width)], g_s.at[0, to, pl.ds(width, width)], mate)
        )

    def finish(k):
        g = rot(k)
        for i in range(2):
            mine = span(g, i * LANES, LANES)
            to = pl.ds(pl.multiple_of(g * rows, rows), rows)
            side = lax.rem(c + i, 2)
            carried = mm(c_s[mine, :], enter_s[...])
            squares = jnp.zeros((LANES, LANES), F32)
            for p in range(tiles):
                cols = pl.ds(p * LANES, LANES)
                val = y_s[mine, cols] + carried[:, p * LANES : (p + 1) * LANES] * ex_s[mine, cols]
                squares = squares + val * val
                g_s[side, to, cols] = (val * gain[:, cols]).astype(BF16)
            sums = jnp.sum(squares, axis=1, keepdims=True)
            row = jnp.sum(jnp.where(eye, sums, 0.0), axis=0, keepdims=True)
            ss_s[g * 2 + i] = jnp.broadcast_to(row, (8, LANES))

    spans = [pl.ds(i * PIECE, PIECE) for i in range(depth // PIECE)]
    first = (len(spans) + 1) // 2
    parts = [spans[:first], spans[first:]]
    part_cols = [pl.ds(0, first * PIECE), pl.ds(first * PIECE, depth - first * PIECE)]

    def product(k, cols):
        mine = pl.ds(pl.multiple_of(rot(k) * rows, rows), rows)
        return mm(g_s[0, mine, :], wo_v[:, cols])

    far = [
        (remote(to_r.at[:, cols], far_r.at[:, cols], right), remote(to_l.at[:, cols], far_l.at[:, cols], left))
        for cols in part_cols
    ]
    plain_r = remote(near_r.at[1], from_l.at[1], right)
    plain_l = remote(near_l.at[0], from_r.at[0], left)
    merged = [
        (
            remote(near_r.at[0, :, cols], from_l.at[0, :, cols], right),
            remote(near_l.at[1, :, cols], from_r.at[1, :, cols], left),
        )
        for cols in part_cols
    ]
    finish(2)
    swaps[0].start()
    finish(1)
    swaps[1].start()
    swaps[0].wait_recv()
    for part, pair in zip(parts, far):
        for cols in part:
            v = product(2, cols).astype(BF16)
            to_r[:, cols] = v[:half]
            to_l[:, cols] = v[half:]
        pair[0].start()
        pair[1].start()
    finish(-1)
    swaps[2].start()
    finish(0)
    swaps[3].start()
    sums = []
    for k in range(1, n):
        copy = remote(ss_s.at[lax.rem(w + k, n)], ss_in.at[w], others[k - 1])
        copy.start()
        sums.append(copy)
    swaps[1].wait_recv()
    for cols in spans:
        v = product(1, cols)
        keep_r[:, cols] = v[:half]
        near_r[1, :, cols] = v[half:].astype(BF16)
    plain_r.start()
    swaps[2].wait_recv()
    for cols in spans:
        v = product(-1, cols)
        near_l[0, :, cols] = v[:half].astype(BF16)
        keep_l[:, cols] = v[half:]
    plain_l.start()
    swaps[3].wait_recv()
    for cols in spans:
        acc[:, cols] = product(0, cols)
    for part, pair, ready in zip(parts, far, merged):
        pair[0].wait_recv()
        for cols in part:
            near_r[0, :, cols] = (keep_r[:, cols] + far_r[:, cols].astype(F32)).astype(BF16)
        ready[0].start()
        pair[1].wait_recv()
        for cols in part:
            near_l[1, :, cols] = (keep_l[:, cols] + far_l[:, cols].astype(F32)).astype(BF16)
        ready[1].start()
    for copy in sums:
        copy.wait_recv()
    ss_in[w] = ss_s[w]
    square = jnp.sum(ss_in[...], axis=0)[0:1, :]
    inverse = lax.rsqrt(square / (width * n) + EPS)
    scale = jnp.sum(jnp.where(eye, inverse, 0.0), axis=1, keepdims=True)
    plain_r.wait_recv()
    plain_l.wait_recv()
    for cols in spans:
        acc[hi_half, cols] = acc[hi_half, cols] + from_l[1, :, cols].astype(F32)
        acc[lo_half, cols] = acc[lo_half, cols] + from_r[0, :, cols].astype(F32)
    for part, pair in zip(parts, merged):
        pair[0].wait_recv()
        pair[1].wait_recv()
        for cols in part:
            v = acc[lo_half, cols] + from_l[0, :, cols].astype(F32)
            out[lo_half, cols] = (v * scale[:half]).astype(BF16)
            v = acc[hi_half, cols] + from_r[1, :, cols].astype(F32)
            out[hi_half, cols] = (v * scale[half:]).astype(BF16)
    assert len(copies) <= COPIES
    for copy in copies:
        if copy is not to_halo:
            copy.wait_send()
    to_halo.wait_send()


def on_device(
    tokens, segments, w_z, w_x, w_dt, w_bc, conv_x, conv_bc, dt_bias, decay_rate, skip_d,
    norm_gain, w_out,
):
    n = lax.axis_size("weight")
    nx, nt = n // 2, lax.axis_size("tm")
    seg = segments.reshape(-1, LANES)
    gain = norm_gain.astype(F32).reshape(1, -1)
    rows, depth = tokens.shape
    width, heads = w_z.shape[1], decay_rate.shape[0]
    block, half = rows * n, rows // 2
    tiles = width // LANES
    wide = width + w_bc.shape[1]
    count = block // GROUP
    hbm, vmem, smem = whole(pl.ANY), whole(), whole(pltpu.SMEM)
    V = pltpu.VMEM
    return pl.pallas_call(
        functools.partial(layer_kernel, nx, nt, heads),
        out_shape=jax.ShapeDtypeStruct((rows, depth), BF16),
        in_specs=[hbm, vmem, hbm, hbm, hbm, vmem, vmem, vmem, vmem, hbm, smem, smem, smem],
        out_specs=vmem,
        scratch_shapes=[
            V((block, depth), BF16),
            V((depth, wide + LANES), BF16),
            V((depth, width), BF16),
            V((8, depth), F32),
            V((2 * width, depth), BF16),
            V((block, width), BF16),
            V((block, wide), BF16),
            V((block, LANES), F32),
            V((HALO, wide), BF16),
            V(seg.shape, jnp.int32),
            V((block + HALO, LANES), F32),
            V((3, block, LANES), F32),
            V((tiles + 2, GROUP, LANES), F32),
            V((tiles + 2, 2 * HALO, LANES), F32),
            V((block, width), BF16),
            V((block, LANES), BF16),
            V((block, LANES), BF16),
            V((block, LANES), F32),
            V((block, LANES), F32),
            V((count, LANES, width), F32),
            V((count, 8, width), F32),
            V((block, width), F32),
            V((block, width), F32),
            V((LANES, width), F32),
            V((8, width), F32),
            V((LANES, width), F32),
            V((8, width), F32),
            V((HOPS, tiles, LANES, LANES), BF16),
            V((HOPS, tiles, LANES, LANES), BF16),
            V((LANES, width), BF16),
            V((2, nx * rows, 2 * width), BF16),
            V((n, 8, LANES), F32),
            V((n, 8, LANES), F32),
            V((half, depth), BF16),
            V((half, depth), BF16),
            V((half, depth), BF16),
            V((half, depth), BF16),
            V((2, half, depth), BF16),
            V((2, half, depth), BF16),
            V((2, half, depth), BF16),
            V((2, half, depth), BF16),
            V((half, depth), F32),
            V((half, depth), F32),
            V((rows, depth), F32),
            pltpu.SemaphoreType.DMA((COPIES,)),
            pltpu.SemaphoreType.DMA((COPIES,)),
            pltpu.SemaphoreType.DMA((5,)),
        ],
        compiler_params=pltpu.CompilerParams(
            collective_id=0, has_side_effects=True, vmem_limit_bytes=VMEM_LIMIT
        ),
        name="layer_block",
    )(
        tokens, seg, w_z, w_x, w_bc, w_dt.T, conv_x, conv_bc, gain, w_out,
        dt_bias, decay_rate, skip_d,
    )


def solution(mesh):
    return jax.shard_map(
        on_device,
        mesh=mesh,
        in_specs=(
            P(("tm", "weight"), None),
            P("tm"),
            P(None, "weight"),
            P(None, "weight"),
            P(None, "weight"),
            P(),
            P(None, "weight"),
            P(),
            P("weight"),
            P("weight"),
            P("weight"),
            P("weight"),
            P("weight", None),
        ),
        out_specs=P(("tm", "weight"), None),
        check_vma=False,
    )
```

time: 353 us -> 83.2 us (0.24)
  the two profiles are of different devices: /device:TPU:25 before, /device:TPU:1 now
where the time goes in v2:
time: 83.2 us; the launch traced here: 83 us
  Pallas kernels  79.7 us (96%)
  local copies, waits for them, and re-layouts  3.21 us (4%)
    pallas_call x1, Pallas kernels, on_device(): pl.pallas_call(functools.partial(layer_kernel, nx, nt, heads), out_shape=...  79.7 us
    unnamed x1, local copies, waits for them, and re-layouts  1.97 us

profile of v2, /device:TPU:1, one launch (start us, length us, event | category | flops | bytes accessed | tf_op | source)
XLA Modules:
  0.0 83.0 jit_solution(4016976623952666520)
XLA Ops:
  0.0 1.2 %reshape.12.gain = f32[1,384]{1,0:T(1,128)} reshape(bf16[384]{0:T(512)(128)(2,1)} %param.24) | data formatting | bytes 2304 | tf_op jit(solution)/shard_map/reshape | solution.py:564
  1.2 79.7 %layer_block.1 = bf16[128,2560]{1,0:T(8,128)(2,1)} custom-call(bf16[128,2560]{1,0:T(8,128)(2,1)} %tok.1, s32[8,128]{1,0:T(8,128)} %bitcast.3, bf16[2560,384]{1,0:T(8,128)(2,1)} %wz.1, bf16[2560,384]{1,0:T(8,128)(2,1)} %wx.1, bf16[2560,256]{1,0:T(8,128)(2,1)} %wbc.1, bf16[6,2560]{1,0:T(8,128)(2,1)} %bitcast.2, f32[4,384]{1,0:T(4,128)} %conv_x.1, ...), custom_call_target="tpu_custom_call" | custom-call | tf_op jit(solution)/shard_map/layer_block/pallas_call | solution.py:573
  81.0 2.0 %copy.15 = bf16[128,2560]{1,0:T(8,128)(2,1)} copy(bf16[128,2560]{1,0:T(8,128)(2,1)} %layer_block.1) | data formatting | bytes 1310720

commit v3 on v2

--- a/solution.py
+++ b/solution.py
@@ -16,7 +16,7 @@
 F32 = jnp.float32
 BF16 = jnp.bfloat16
 MESH = pl.DeviceIdType.MESH
-VMEM_LIMIT = 56 * 1024 * 1024
+VMEM_LIMIT = 62 * 1024 * 1024
 COPIES = 64
 
 
@@ -35,9 +35,9 @@
 
 def layer_kernel(
     nx, nt, heads,
-    tok, seg, wz, wx, wbc, wdt, conv_x, conv_bc, gain, wo, bias, rate, skip,
-    out,
-    buf, wa_v, wz_v, wd_f, wo_v, z_s, xbc_s, dt_s, halo_s, seg_s,
+    tok, seg_h, wz, wx, wbc, wdt_h, conv_x_h, conv_bc_h, gain_h, wo, bias_h, rate_h, skip_h,
+    out_h,
+    seg, wdt, conv_x, conv_bc, gain_v, bias, rate, skip, out, buf, wa_v, wz_v, wd_f, wo_v, z_s, xbc_s, dt_s, halo_s, seg_s,
     segc, mask_s, cv_s, cvh_s, xs_s, b_s, c_s, logs_s, dts_s, fresh_s, keep_s, y_s, ex_s, local_s, decay_s,
     ssm_s, kcum_s, hop_out, hop_in, enter_s, g_s, ss_s, ss_in,
     to_r, to_l, far_r, far_l, near_r, near_l, from_l, from_r, keep_r, keep_l, acc,
@@ -85,6 +85,17 @@
 
     own = pltpu.make_async_copy(tok, chunk(x), local.at[0])
     own.start()
+    smalls = [
+        pltpu.make_async_copy(src, dst, local.at[5 + i])
+        for i, (src, dst) in enumerate(
+            [
+                (seg_h, seg), (wdt_h, wdt), (conv_x_h, conv_x), (conv_bc_h, conv_bc),
+                (gain_h, gain_v), (bias_h, bias), (rate_h, rate), (skip_h, skip),
+            ]
+        )
+    ]
+    for load in smalls:
+        load.start()
     loads = [
         pltpu.make_async_copy(wx, wa_v.at[:, pl.ds(0, width)], local.at[1]),
         pltpu.make_async_copy(wbc, wa_v.at[:, pl.ds(width, wbc.shape[1])], local.at[2]),
@@ -96,9 +107,21 @@
     load_wo.start()
     others = [{"tm": t, "weight": lax.rem(w + k, n)} for k in range(1, n)]
     barrier = pltpu.get_barrier_semaphore()
-    for device in others + [before]:
+    for device in others:
         pl.semaphore_signal(barrier, inc=1, device_id=device, device_id_type=MESH)
-    pl.semaphore_wait(barrier, n)
+    inner, outer = t > 0, t < nt - 1
+
+    @pl.when(inner)
+    def _():
+        pl.semaphore_signal(barrier, inc=1, device_id=before, device_id_type=MESH)
+
+    pl.semaphore_wait(barrier, jnp.where(outer, n, n - 1))
+
+    def when_outer(act):
+        pl.when(outer)(act)
+
+    def when_inner(act):
+        pl.when(inner)(act)
 
     xl, xr, xf = rot(-1), rot(1), rot(2)
     lo_half, hi_half = pl.ds(0, half), pl.ds(half, half)
@@ -107,9 +130,10 @@
     a_l1 = remote(tok.at[hi_half], chunk(x, half, half), left)
     a_r1 = remote(tok.at[hi_half], chunk(x, half, half), right)
     a_l0 = remote(tok.at[lo_half], chunk(x, 0, half), left)
-    to_seg = remote(seg, seg_s, after)
-    for copy in (m0, a_r0, a_l1, a_r1, a_l0, to_seg):
+    to_seg = remote(seg_h, seg_s, after)
+    for copy in (m0, a_r0, a_l1, a_r1, a_l0):
         copy.start()
+    when_outer(to_seg.start)
     to_wo = remote(wo, wo_v.at[pl.ds(width, width)], mate)
     to_wo.start()
     relay_r = [same_place(xl, q * quarter, quarter, right) for q in (0, 1)]
@@ -122,6 +146,16 @@
     ]
     to_halo = remote(xbc_s.at[pl.ds(block - HALO, HALO)], halo_s, after)
 
+    for load in smalls:
+        load.wait()
+    gain = gain_v[...].astype(F32).reshape(1, width)
+
+    @pl.when(t == 0)
+    def _():
+        seg_s[...] = jnp.zeros_like(seg_s)
+        halo_s[...] = jnp.zeros_like(halo_s)
+        hop_in[...] = jnp.zeros_like(hop_in)
+
     wd_f[...] = jnp.zeros_like(wd_f)
     wd_f[pl.ds(0, heads), :] = wdt[...].astype(F32)
     for i in range(depth // LANES):
@@ -154,7 +188,7 @@
             row = jnp.where(lane >= q * head_dim, skip[p * per + q], row)
         skip_rows.append(row)
 
-    to_seg.wait_recv()
+    when_inner(to_seg.wait_recv)
     old = columns(seg_s[pl.ds(seg_s.shape[0] - 1, 1), :])
     old = jnp.where(t == 0, -1.0, old)
     segc[pl.ds(0, HALO), :] = old[LANES - HALO :, :]
@@ -178,7 +212,7 @@
         dt_s[mine, :] = v[:, 128:].astype(F32)
 
     def halo_if_last(g):
-        @pl.when(g == nx - 1)
+        @pl.when((g == nx - 1) & outer)
         def _():
             to_halo.start()
 
@@ -360,7 +394,7 @@
     steps(xr)
 
     def halo_wait(places):
-        @pl.when(places)
+        @pl.when(places & inner)
         def _():
             to_halo.wait_recv()
 
@@ -402,15 +436,15 @@
         local_s[:, cols] = total
         decay_s[:, cols] = decay
         hop_out[0, p] = total.astype(BF16)
-        hops[0][p].start()
+        when_outer(hops[0][p].start)
 
     def hop_on(h):
         for p in range(tiles):
             cols = pl.ds(p * LANES, LANES)
-            hops[h - 1][p].wait_recv()
+            when_inner(hops[h - 1][p].wait_recv)
             total = local_s[:, cols] + decay_s[0:1, cols] * hop_in[h - 1, p].astype(F32)
             hop_out[h, p] = total.astype(BF16)
-            hops[h][p].start()
+            when_outer(hops[h][p].start)
 
     ssm_s[...] = jnp.zeros_like(ssm_s)
     kcum_s[...] = jnp.ones_like(kcum_s)
@@ -423,13 +457,13 @@
     project_z(xf)
     lax.fori_loop(0, 1, mix_step, 0)
     hop_on(1)
-    lax.fori_loop(1, 3, mix_step, 0)
+    lax.fori_loop(1, 2, mix_step, 0)
     hop_on(2)
-    lax.fori_loop(3, nx, mix_step, 0)
+    lax.fori_loop(2, nx, mix_step, 0)
     load_wo.wait()
     to_wo.wait_recv()
     for p in range(tiles):
-        hops[HOPS - 1][p].wait_recv()
+        when_inner(hops[HOPS - 1][p].wait_recv)
         enter_s[:, pl.ds(p * LANES, LANES)] = hop_in[HOPS - 1, p]
 
     eye = (
@@ -444,22 +478,24 @@
             remote(g_s.at[1, to, pl.ds(0, width)], g_s.at[0, to, pl.ds(width, width)], mate)
         )
 
-    def finish(k):
+    def finish(k, swap):
         g = rot(k)
-        for i in range(2):
+        for side in (1, 0):
+            i = lax.rem(c + side, 2)
             mine = span(g, i * LANES, LANES)
             to = pl.ds(pl.multiple_of(g * rows, rows), rows)
-            side = lax.rem(c + i, 2)
             carried = mm(c_s[mine, :], enter_s[...])
             squares = jnp.zeros((LANES, LANES), F32)
             for p in range(tiles):
                 cols = pl.ds(p * LANES, LANES)
                 val = y_s[mine, cols] + carried[:, p * LANES : (p + 1) * LANES] * ex_s[mine, cols]
                 squares = squares + val * val
-                g_s[side, to, cols] = (val * gain[:, cols]).astype(BF16)
+                g_s[side, to, cols] = (val * gain[:, p * LANES : (p + 1) * LANES]).astype(BF16)
             sums = jnp.sum(squares, axis=1, keepdims=True)
             row = jnp.sum(jnp.where(eye, sums, 0.0), axis=0, keepdims=True)
             ss_s[g * 2 + i] = jnp.broadcast_to(row, (8, LANES))
+            if side == 1:
+                swap.start()
 
     spans = [pl.ds(i * PIECE, PIECE) for i in range(depth // PIECE)]
     first = (len(spans) + 1) // 2
@@ -483,10 +519,8 @@
         )
         for cols in part_cols
     ]
-    finish(2)
-    swaps[0].start()
-    finish(1)
-    swaps[1].start()
+    finish(2, swaps[0])
+    finish(1, swaps[1])
     swaps[0].wait_recv()
     for part, pair in zip(parts, far):
         for cols in part:
@@ -495,10 +529,8 @@
             to_l[:, cols] = v[half:]
         pair[0].start()
         pair[1].start()
-    finish(-1)
-    swaps[2].start()
-    finish(0)
-    swaps[3].start()
+    finish(-1, swaps[2])
+    finish(0, swaps[3])
     sums = []
     for k in range(1, n):
         copy = remote(ss_s.at[lax.rem(w + k, n)], ss_in.at[w], others[k - 1])
@@ -539,7 +571,11 @@
     for cols in spans:
         acc[hi_half, cols] = acc[hi_half, cols] + from_l[1, :, cols].astype(F32)
         acc[lo_half, cols] = acc[lo_half, cols] + from_r[0, :, cols].astype(F32)
-    for part, pair in zip(parts, merged):
+    stores = [
+        pltpu.make_async_copy(out.at[:, cols], out_h.at[:, cols], local.at[13 + i])
+        for i, cols in enumerate(part_cols)
+    ]
+    for i, (part, pair) in enumerate(zip(parts, merged)):
         pair[0].wait_recv()
         pair[1].wait_recv()
         for cols in part:
@@ -547,11 +583,20 @@
             out[lo_half, cols] = (v * scale[:half]).astype(BF16)
             v = acc[hi_half, cols] + from_r[1, :, cols].astype(F32)
             out[hi_half, cols] = (v * scale[half:]).astype(BF16)
+        stores[i].start()
     assert len(copies) <= COPIES
+    along = [to_seg, to_halo] + [hop for row in hops for hop in row]
     for copy in copies:
-        if copy is not to_halo:
+        if all(copy is not other for other in along):
             copy.wait_send()
-    to_halo.wait_send()
+
+    @pl.when(outer)
+    def _():
+        for copy in along:
+            copy.wait_send()
+
+    for store in stores:
+        store.wait()
 
 
 def on_device(
@@ -561,21 +606,29 @@
     n = lax.axis_size("weight")
     nx, nt = n // 2, lax.axis_size("tm")
     seg = segments.reshape(-1, LANES)
-    gain = norm_gain.astype(F32).reshape(1, -1)
     rows, depth = tokens.shape
     width, heads = w_z.shape[1], decay_rate.shape[0]
     block, half = rows * n, rows // 2
     tiles = width // LANES
     wide = width + w_bc.shape[1]
     count = block // GROUP
-    hbm, vmem, smem = whole(pl.ANY), whole(), whole(pltpu.SMEM)
+    hbm = whole(pl.ANY)
     V = pltpu.VMEM
     return pl.pallas_call(
         functools.partial(layer_kernel, nx, nt, heads),
         out_shape=jax.ShapeDtypeStruct((rows, depth), BF16),
-        in_specs=[hbm, vmem, hbm, hbm, hbm, vmem, vmem, vmem, vmem, hbm, smem, smem, smem],
-        out_specs=vmem,
+        in_specs=[whole(pltpu.HBM)] * 13,
+        out_specs=hbm,
         scratch_shapes=[
+            V(seg.shape, jnp.int32),
+            V((heads, depth), BF16),
+            V(conv_x.shape, F32),
+            V(conv_bc.shape, F32),
+            V((width,), BF16),
+            pltpu.SMEM((heads,), F32),
+            pltpu.SMEM((heads,), F32),
+            pltpu.SMEM((heads,), F32),
+            V((rows, depth), BF16),
             V((block, depth), BF16),
             V((depth, wide + LANES), BF16),
             V((depth, width), BF16),
@@ -622,14 +675,14 @@
             V((rows, depth), F32),
             pltpu.SemaphoreType.DMA((COPIES,)),
             pltpu.SemaphoreType.DMA((COPIES,)),
-            pltpu.SemaphoreType.DMA((5,)),
+            pltpu.SemaphoreType.DMA((15,)),
         ],
         compiler_params=pltpu.CompilerParams(
             collective_id=0, has_side_effects=True, vmem_limit_bytes=VMEM_LIMIT
         ),
         name="layer_block",
     )(
-        tokens, seg, w_z, w_x, w_bc, w_dt.T, conv_x, conv_bc, gain, w_out,
+        tokens, seg, w_z, w_x, w_bc, w_dt.T, conv_x, conv_bc, norm_gain, w_out,
         dt_bias, decay_rate, skip_d,
     )
 

time: 83.2 us -> 78.3 us (0.941)
  the two profiles are of different devices: /device:TPU:1 before, /device:TPU:25 now
where the time goes in v3:
time: 78.3 us; the launch traced here: 78.2 us
  Pallas kernels  76.2 us (97%)
  local copies, waits for them, and re-layouts  1.97 us (3%)
    pallas_call x1, Pallas kernels, on_device(): pl.pallas_call(functools.partial(layer_kernel, nx, nt, heads), out_shape=...  76.2 us
    unnamed x1, local copies, waits for them, and re-layouts  1.97 us

profile of v3, /device:TPU:25, one launch (start us, length us, event | category | flops | bytes accessed | tf_op | source)
XLA Modules:
  0.0 78.2 jit_solution(15428146643270817649)
XLA Ops:
  0.0 76.2 %layer_block.1 = bf16[128,2560]{1,0:T(8,128)(2,1)} custom-call(bf16[128,2560]{1,0:T(8,128)(2,1)} %tok.1, s32[8,128]{1,0:T(8,128)} %bitcast.3, bf16[2560,384]{1,0:T(8,128)(2,1)} %wz.1, bf16[2560,384]{1,0:T(8,128)(2,1)} %wx.1, bf16[2560,256]{1,0:T(8,128)(2,1)} %wbc.1, bf16[6,2560]{1,0:T(8,128)(2,1)} %bitcast.2, f32[4,384]{1,0:T(4,128)} %conv_x_h.1, ...), custom_call_target="tpu_custom_call" | custom-call | tf_op jit(solution)/shard_map/layer_block/pallas_call | solution.py:617
  76.2 2.0 %copy.15 = bf16[128,2560]{1,0:T(8,128)(2,1)} copy(bf16[128,2560]{1,0:T(8,128)(2,1)} %layer_block.1) | data formatting | bytes 1310720

commit v4 on v3

--- a/solution.py
+++ b/solution.py
@@ -11,13 +11,14 @@
 LANES = 128
 HALO = 16
 HOPS = 3
+PARTS = 4
 PIECE = 256
 EPS = 1e-5
 F32 = jnp.float32
 BF16 = jnp.bfloat16
 MESH = pl.DeviceIdType.MESH
 VMEM_LIMIT = 62 * 1024 * 1024
-COPIES = 64
+COPIES = 80
 
 
 def whole(space=pltpu.VMEM):
@@ -211,6 +212,31 @@
         xbc_s[mine, pl.ds(512, 128)] = v[:, :128]
         dt_s[mine, :] = v[:, 128:].astype(F32)
 
+    halves = [[(0, half), (rows, half)], [(half, half), (rows + half, half)]]
+    quarters = [[(i * half + q * quarter, quarter) for i in range(4)] for q in range(2)]
+
+    def some_rows(g, slices):
+        mine = [span(g, *item) for item in slices]
+        return mine, jnp.concatenate([buf[m, :] for m in mine], axis=0)
+
+    def some_store(ref, mine, cols, v):
+        size = v.shape[0] // len(mine)
+        for i, m in enumerate(mine):
+            ref[m, cols] = v[i * size : (i + 1) * size].astype(ref.dtype)
+
+    def project_some(g, slices):
+        mine, lhs = some_rows(g, slices)
+        some_store(xbc_s, mine, pl.ds(0, 256), mm(lhs, wa_v[:, pl.ds(0, 256)]).astype(BF16))
+        some_store(xbc_s, mine, pl.ds(256, 256), mm(lhs, wa_v[:, pl.ds(256, 256)]).astype(BF16))
+        v = mm(lhs, wa_v[:, pl.ds(512, 256)]).astype(BF16)
+        some_store(xbc_s, mine, pl.ds(512, 128), v[:, :128])
+        some_store(dt_s, mine, pl.ds(0, 128), v[:, 128:])
+
+    def project_z_some(g, slices):
+        mine, lhs = some_rows(g, slices)
+        some_store(z_s, mine, pl.ds(0, 256), mm(lhs, wz_v[:, pl.ds(0, 256)]).astype(BF16))
+        some_store(z_s, mine, pl.ds(256, 128), mm(lhs, wz_v[:, pl.ds(256, 128)]).astype(BF16))
+
     def halo_if_last(g):
         @pl.when((g == nx - 1) & outer)
         def _():
@@ -243,13 +269,13 @@
         total = total + source[pl.ds(HALO, size), :] * taps[3:4, :]
         conv_store(j, mine, silu(total).astype(BF16))
 
-    def conv_main(g):
-        for j in range(tiles + 2):
+    def conv_main(g, tiles_of=tuple(range(width // LANES + 2))):
+        for j in tiles_of:
             cv_s[j] = xbc_s[span(g), pl.ds(j * LANES, LANES)].astype(F32)
             conv_rows(j, cv_s.at[j], g, HALO, GROUP - HALO)
 
-    def conv_head(g):
-        for j in range(tiles + 2):
+    def conv_head(g, tiles_of=tuple(range(width // LANES + 2))):
+        for j in tiles_of:
             cols = pl.ds(j * LANES, LANES)
             back = pl.ds(pl.multiple_of(jnp.maximum(g * GROUP - HALO, 0), HALO), HALO)
 
@@ -262,7 +288,7 @@
                 cvh_s[j, pl.ds(0, HALO), :] = xbc_s[back, cols].astype(F32)
 
             cvh_s[j, pl.ds(HALO, HALO), :] = xbc_s[span(g, 0, HALO), cols].astype(F32)
-        for j in range(tiles + 2):
+        for j in tiles_of:
             conv_rows(j, cvh_s.at[j], g, 0, HALO)
 
     low_ones = (
@@ -372,18 +398,23 @@
     a_l1.wait_recv()
     for copy in relay_r + relay_l + [fwd_l0, fwd_r1]:
         copy.start()
+    fwd_l0.wait_recv()
+    project_some(xl, halves[0])
+    project_z_some(xl, halves[0])
+    fwd_r1.wait_recv()
+    project_some(xr, halves[1])
+    halo_if_last(xr)
+    project_z_some(xr, halves[1])
     a_r1.wait_recv()
     fwd_l1.start()
     a_l0.wait_recv()
     fwd_r0.start()
-    fwd_l0.wait_recv()
     fwd_l1.wait_recv()
-    project_xbc(xl)
+    project_some(xl, halves[1])
     halo_if_last(xl)
-    fwd_r1.wait_recv()
     fwd_r0.wait_recv()
-    project_xbc(xr)
-    halo_if_last(xr)
+    project_some(xr, halves[0])
+    project_z_some(xr, halves[0])
     relay_r[0].wait_recv()
     fwd_f[0][0].start()
     relay_l[0].wait_recv()
@@ -401,6 +432,7 @@
     halo_wait((x == 0) | (x == nx - 1))
 
     conv_head(xr)
+    project_z_some(xl, halves[1])
     relay_r[1].wait_recv()
     fwd_f[1][0].start()
     relay_l[1].wait_recv()
@@ -408,19 +440,18 @@
     state(xr)
     conv_head(x)
     state(x)
-    project_z(xl)
-    for pair in fwd_f:
+    for slices, pair in zip(quarters, fwd_f):
         for copy in pair:
             copy.wait_recv()
-    project_xbc(xf)
+        project_some(xf, slices)
     halo_if_last(xf)
-    conv_main(xf)
+    conv_main(xf, tuple(range(tiles + 1)))
     steps(xf)
     halo_wait(x == 2)
-    conv_head(xf)
+    conv_head(xf, tuple(range(tiles + 1)))
     state(xf)
     halo_wait(x == 1)
-    conv_head(xl)
+    conv_head(xl, tuple(range(tiles + 1)))
     state(xl)
 
     hops = [
@@ -453,7 +484,9 @@
         mix(g)
         return carry
 
-    project_z(xr)
+    conv_main(xf, (tiles + 1,))
+    conv_head(xf, (tiles + 1,))
+    conv_head(xl, (tiles + 1,))
     project_z(xf)
     lax.fori_loop(0, 1, mix_step, 0)
     hop_on(1)
@@ -498,9 +531,9 @@
                 swap.start()
 
     spans = [pl.ds(i * PIECE, PIECE) for i in range(depth // PIECE)]
-    first = (len(spans) + 1) // 2
-    parts = [spans[:first], spans[first:]]
-    part_cols = [pl.ds(0, first * PIECE), pl.ds(first * PIECE, depth - first * PIECE)]
+    bounds = [len(spans) * i // PARTS for i in range(PARTS + 1)]
+    parts = [spans[i:j] for i, j in zip(bounds, bounds[1:])]
+    part_cols = [pl.ds(i * PIECE, (j - i) * PIECE) for i, j in zip(bounds, bounds[1:])]
 
     def product(k, cols):
         mine = pl.ds(pl.multiple_of(rot(k) * rows, rows), rows)
@@ -675,7 +708,7 @@
             V((rows, depth), F32),
             pltpu.SemaphoreType.DMA((COPIES,)),
             pltpu.SemaphoreType.DMA((COPIES,)),
-            pltpu.SemaphoreType.DMA((15,)),
+            pltpu.SemaphoreType.DMA((13 + PARTS,)),
         ],
         compiler_params=pltpu.CompilerParams(
             collective_id=0, has_side_effects=True, vmem_limit_bytes=VMEM_LIMIT

time: 78.3 us -> 77.7 us (level)
  no operation moved by 1% of the time
where the time goes in v4:
time: 77.7 us; the launch traced here: 77.6 us
  Pallas kernels  75.6 us (97%)
  local copies, waits for them, and re-layouts  1.97 us (3%)
    pallas_call x1, Pallas kernels, on_device(): pl.pallas_call(functools.partial(layer_kernel, nx, nt, heads), out_shape=...  75.6 us
    unnamed x1, local copies, waits for them, and re-layouts  1.97 us

profile of v4, /device:TPU:25, one launch (start us, length us, event | category | flops | bytes accessed | tf_op | source)
XLA Modules:
  0.0 77.6 jit_solution(4215233231242727148)
XLA Ops:
  0.0 75.6 %layer_block.1 = bf16[128,2560]{1,0:T(8,128)(2,1)} custom-call(bf16[128,2560]{1,0:T(8,128)(2,1)} %tok.1, s32[8,128]{1,0:T(8,128)} %bitcast.3, bf16[2560,384]{1,0:T(8,128)(2,1)} %wz.1, bf16[2560,384]{1,0:T(8,128)(2,1)} %wx.1, bf16[2560,256]{1,0:T(8,128)(2,1)} %wbc.1, bf16[6,2560]{1,0:T(8,128)(2,1)} %bitcast.2, f32[4,384]{1,0:T(4,128)} %conv_x_h.1, ...), custom_call_target="tpu_custom_call" | custom-call | tf_op jit(solution)/shard_map/layer_block/pallas_call | solution.py:650
  75.6 2.0 %copy.15 = bf16[128,2560]{1,0:T(8,128)(2,1)} copy(bf16[128,2560]{1,0:T(8,128)(2,1)} %layer_block.1) | data formatting | bytes 1310720

commit v5 on v4

--- a/solution.py
+++ b/solution.py
@@ -42,7 +42,7 @@
     segc, mask_s, cv_s, cvh_s, xs_s, b_s, c_s, logs_s, dts_s, fresh_s, keep_s, y_s, ex_s, local_s, decay_s,
     ssm_s, kcum_s, hop_out, hop_in, enter_s, g_s, ss_s, ss_in,
     to_r, to_l, far_r, far_l, near_r, near_l, from_l, from_r, keep_r, keep_l, acc,
-    send, recv, local,
+    send, recv, local, ready,
 ):
     t = lax.axis_index("tm")
     w = lax.axis_index("weight")
@@ -112,11 +112,11 @@
         pl.semaphore_signal(barrier, inc=1, device_id=device, device_id_type=MESH)
     inner, outer = t > 0, t < nt - 1
 
-    @pl.when(inner)
+    @pl.when(outer)
     def _():
-        pl.semaphore_signal(barrier, inc=1, device_id=before, device_id_type=MESH)
-
-    pl.semaphore_wait(barrier, jnp.where(outer, n, n - 1))
+        pl.semaphore_signal(barrier, inc=1, device_id=after, device_id_type=MESH)
+
+    pl.semaphore_wait(barrier, jnp.where(inner, n, n - 1))
 
     def when_outer(act):
         pl.when(outer)(act)
@@ -134,7 +134,11 @@
     to_seg = remote(seg_h, seg_s, after)
     for copy in (m0, a_r0, a_l1, a_r1, a_l0):
         copy.start()
-    when_outer(to_seg.start)
+
+    @pl.when(inner)
+    def _():
+        pl.semaphore_signal(ready, inc=1, device_id=before, device_id_type=MESH)
+
     to_wo = remote(wo, wo_v.at[pl.ds(width, width)], mate)
     to_wo.start()
     relay_r = [same_place(xl, q * quarter, quarter, right) for q in (0, 1)]
@@ -146,6 +150,11 @@
         for q in (0, 1)
     ]
     to_halo = remote(xbc_s.at[pl.ds(block - HALO, HALO)], halo_s, after)
+
+    @pl.when(outer)
+    def _():
+        pl.semaphore_wait(ready, 1)
+        to_seg.start()
 
     for load in smalls:
         load.wait()
@@ -709,6 +718,7 @@
             pltpu.SemaphoreType.DMA((COPIES,)),
             pltpu.SemaphoreType.DMA((COPIES,)),
             pltpu.SemaphoreType.DMA((13 + PARTS,)),
+            pltpu.SemaphoreType.REGULAR,
         ],
         compiler_params=pltpu.CompilerParams(
             collective_id=0, has_side_effects=True, vmem_limit_bytes=VMEM_LIMIT

time: 77.7 us -> 77.5 us (level)
  no operation moved by 1% of the time
where the time goes in v5:
time: 77.5 us; the launch traced here: 77.4 us
  Pallas kernels  75.4 us (97%)
  local copies, waits for them, and re-layouts  1.97 us (3%)
    pallas_call x1, Pallas kernels, on_device(): pl.pallas_call(functools.partial(layer_kernel, nx, nt, heads), out_shape=...  75.4 us
    unnamed x1, local copies, waits for them, and re-layouts  1.97 us

profile of v5, /device:TPU:25, one launch (start us, length us, event | category | flops | bytes accessed | tf_op | source)
XLA Modules:
  0.0 77.4 jit_solution(4366092040762516581)
XLA Ops:
  0.0 75.4 %layer_block.1 = bf16[128,2560]{1,0:T(8,128)(2,1)} custom-call(bf16[128,2560]{1,0:T(8,128)(2,1)} %tok.1, s32[8,128]{1,0:T(8,128)} %bitcast.3, bf16[2560,384]{1,0:T(8,128)(2,1)} %wz.1, bf16[2560,384]{1,0:T(8,128)(2,1)} %wx.1, bf16[2560,256]{1,0:T(8,128)(2,1)} %wbc.1, bf16[6,2560]{1,0:T(8,128)(2,1)} %bitcast.2, f32[4,384]{1,0:T(4,128)} %conv_x_h.1, ...), custom_call_target="tpu_custom_call" | custom-call | tf_op jit(solution)/shard_map/layer_block/pallas_call | solution.py:659
  75.4 2.0 %copy.15 = bf16[128,2560]{1,0:T(8,128)(2,1)} copy(bf16[128,2560]{1,0:T(8,128)(2,1)} %layer_block.1) | data formatting | bytes 1310720

commit v6 on v5

--- a/solution.py
+++ b/solution.py
@@ -423,7 +423,6 @@
     halo_if_last(xl)
     fwd_r0.wait_recv()
     project_some(xr, halves[0])
-    project_z_some(xr, halves[0])
     relay_r[0].wait_recv()
     fwd_f[0][0].start()
     relay_l[0].wait_recv()
@@ -441,7 +440,6 @@
     halo_wait((x == 0) | (x == nx - 1))
 
     conv_head(xr)
-    project_z_some(xl, halves[1])
     relay_r[1].wait_recv()
     fwd_f[1][0].start()
     relay_l[1].wait_recv()
@@ -496,6 +494,8 @@
     conv_main(xf, (tiles + 1,))
     conv_head(xf, (tiles + 1,))
     conv_head(xl, (tiles + 1,))
+    project_z_some(xr, halves[0])
+    project_z_some(xl, halves[1])
     project_z(xf)
     lax.fori_loop(0, 1, mix_step, 0)
     hop_on(1)

time: 77.5 us -> 77.5 us (level)
  no operation moved by 1% of the time
where the time goes in v6:
time: 77.5 us; the launch traced here: 77.3 us
  Pallas kernels  75.4 us (97%)
  local copies, waits for them, and re-layouts  1.97 us (3%)
    pallas_call x1, Pallas kernels, on_device(): pl.pallas_call(functools.partial(layer_kernel, nx, nt, heads), out_shape=...  75.4 us
    unnamed x1, local copies, waits for them, and re-layouts  1.97 us

profile of v6, /device:TPU:25, one launch (start us, length us, event | category | flops | bytes accessed | tf_op | source)
XLA Modules:
  0.0 77.3 jit_solution(16644811631103829760)
XLA Ops:
  0.0 75.4 %layer_block.1 = bf16[128,2560]{1,0:T(8,128)(2,1)} custom-call(bf16[128,2560]{1,0:T(8,128)(2,1)} %tok.1, s32[8,128]{1,0:T(8,128)} %bitcast.3, bf16[2560,384]{1,0:T(8,128)(2,1)} %wz.1, bf16[2560,384]{1,0:T(8,128)(2,1)} %wx.1, bf16[2560,256]{1,0:T(8,128)(2,1)} %wbc.1, bf16[6,2560]{1,0:T(8,128)(2,1)} %bitcast.2, f32[4,384]{1,0:T(4,128)} %conv_x_h.1, ...), custom_call_target="tpu_custom_call" | custom-call | tf_op jit(solution)/shard_map/layer_block/pallas_call | solution.py:659
  75.4 2.0 %copy.15 = bf16[128,2560]{1,0:T(8,128)(2,1)} copy(bf16[128,2560]{1,0:T(8,128)(2,1)} %layer_block.1) | data formatting | bytes 1310720
